TPU v7x, 32 devices: a whole 2x2x4 slice. The times are simulated.
32 devices in a mesh: gx: 2 (over x), gy: 4 (over z), lev: 4 (over y, core).
Axes of the slice: x: 2, y: 2, z: 4, core: 2. Of those that a mesh axis runs over, the one named last changes fastest.
Arguments:
- zonal: float32 [128, 64, 512], P('lev', 'gx', 'gy'), may hold values from -6 to 6
- meridional: float32 [128, 64, 512], P('lev', 'gx', 'gy'), may hold values from -6 to 6
- vertical: float32 [128, 64, 512], P('lev', 'gx', 'gy'), may hold values from -4 to 4
- pressure: float32 [128, 64, 512], P('lev', 'gx', 'gy'), may hold values from -6 to 6
- coupling: float32 [128, 64, 512], P('lev', 'gx', 'gy'), may hold values from 0.125 to 32768
- surface: int32 [64, 512], P('gx', 'gy'), may hold values from 0 to 16
- lid_flag: int32 [64, 512], P('gx', 'gy'), may hold values from 0 to 1
Outputs:
- zonal_out: float32 [128, 64, 512], P('lev', 'gx', 'gy')
- meridional_out: float32 [128, 64, 512], P('lev', 'gx', 'gy')
- vertical_out: float32 [128, 64, 512], P('lev', 'gx', 'gy')
- pressure_out: float32 [128, 64, 512], P('lev', 'gx', 'gy')
Inputs may be any that keep to these rules, and one draw needn't show every extreme that they name: `surface`: the number of lowest levels of a column that lie below the terrain. `lid_flag`: 1 closes the column's top with a rigid lid, 0 leaves it open.
All inputs are finite; a program needn't handle non-finite values.
Results may differ from a plain program's by a relative error of at most 0.0003.
Values sent between devices are 32-bit elements; how exact they have to be, the bound alone decides.
No kernel may reach another device: no remote copies, remote signals or barrier semaphores. Data moves between devices by JAX's collectives and lax.ppermute only.
A program may use at most 128 MiB of HBM per device.

v0:
```python
import functools

import jax
import jax.numpy as jnp
from jax import lax
from jax.experimental import pallas as pl
from jax.experimental.pallas import tpu as pltpu
from jax.sharding import PartitionSpec as P

SUBSTEPS = 3
H_STEP = 0.25
D_STEP = 0.25
V_STEP = 0.5
P_STEP = 0.5
F32 = jnp.float32
PAD = 8

VMEM = pl.BlockSpec(memory_space=pltpu.VMEM)
HBM = pl.BlockSpec(memory_space=pltpu.HBM)


def call(kernel, outs, args, scratch=(), spaces=None, out_spaces=None, types=()):
    return list(
        pl.pallas_call(
            kernel,
            out_shape=[jax.ShapeDtypeStruct(s, types[n] if n < len(types) else F32) for n, s in enumerate(outs)],
            in_specs=spaces or [VMEM] * len(args),
            out_specs=out_spaces or [VMEM] * len(outs),
            scratch_shapes=list(scratch),
            compiler_params=pltpu.CompilerParams(vmem_limit_bytes=20 * 1024 * 1024),
        )(*args)
    )


class Halo:
    def __init__(self, axis, plane):
        self.axis, self.plane = axis, plane
        self.n = lax.axis_size(axis)
        self.count = 1 if self.n <= 2 else 2
        self.swap = self.n > 2 and self.n % 2 == 0

    def shapes(self, rows):
        return [(2 * rows,) + self.plane] if self.count == 1 else [(rows,) + self.plane] * 2

    def scratch(self, rows):
        return pltpu.VMEM((2, rows) + self.plane, F32)

    def write(self, refs, both, even):
        rows = both.shape[1]
        if self.count == 1:
            refs[0][:rows] = both[0]
            refs[0][rows:] = both[1]
        elif self.swap:
            refs[0][...] = jnp.where(even, both[0], both[1])
            refs[1][...] = jnp.where(even, both[1], both[0])
        else:
            refs[0][...] = both[0]
            refs[1][...] = both[1]

    def up(self, refs, r, even):
        if self.swap:
            return jnp.where(even, refs[0][r], refs[1][r])
        return refs[0][r]

    def down(self, refs, r, even):
        if self.swap:
            return jnp.where(even, refs[1][r], refs[0][r])
        return refs[0][refs[0].shape[0] // 2 + r] if self.count == 1 else refs[1][r]

    def low(self, refs, r, even):
        if self.swap:
            return jnp.where(even, refs[1][r], refs[0][r])
        return refs[0][r]

    def high(self, refs, r, even):
        if self.swap:
            return jnp.where(even, refs[0][r], refs[1][r])
        return refs[0][refs[0].shape[0] // 2 + r] if self.count == 1 else refs[1][r]

    def exchange(self, messages):
        n = self.n
        if n == 1:
            return messages
        if self.swap:
            first = [(i, i ^ 1) for i in range(n)]
            second = [(i, (i + 1) % n if i % 2 else (i - 1) % n) for i in range(n)]
            got = lax.ppermute(messages[1], self.axis, second)
            return [lax.ppermute(messages[0], self.axis, first), got]
        up = [(i, (i + 1) % n) for i in range(n)]
        if n == 2:
            return [lax.ppermute(messages[0], self.axis, up)]
        down = [(j, i) for i, j in up]
        return [lax.ppermute(messages[0], self.axis, up), lax.ppermute(messages[1], self.axis, down)]


def to_lev(message, m):
    n = lax.axis_size("lev")
    if n & (n - 1) == 0:
        return lax.ppermute(message, "lev", [(i, i ^ m) for i in range(n)])
    return lax.ppermute(message, "lev", [(i, (i + m) % n) for i in range(n)])


def source_of(group, m, n):
    return group ^ m if n & (n - 1) == 0 else (group - m) % n


def pack_columns(ref, picks, outs):
    depth, ni, nj = ref.shape
    per = nj // ni
    for b in range(depth // per):
        turned = ref[b * per : (b + 1) * per].reshape(per * ni, nj).T
        for c, out in zip(picks, outs):
            out[b : b + 1, :] = turned[c : c + 1, :]


def pack_pressure(press, both_x, both_y):
    ni, nj = press.shape[1:]
    for r in range(2):
        both_x[0, r] = press[:, ni - 2 + r, :]
        both_x[1, r] = press[:, r, :]
    pack_columns(press, (nj - 2, nj - 1, 0, 1), (both_y.at[0, 0], both_y.at[0, 1], both_y.at[1, 0], both_y.at[1, 1]))


def first_kernel(hx, hy, *refs):
    refs = list(refs)
    take = lambda n: [refs.pop(0) for _ in range(n)]
    sources, targets = take(6), take(6)
    mx, my = take(hx.count), take(hy.count)
    both_x, both_y, sems = refs
    p, v, u = targets[:3]
    copies = [pltpu.make_async_copy(a, b, sems.at[n]) for n, (a, b) in enumerate(zip(sources, targets))]
    for copy in copies:
        copy.start()
    ni, nj = p.shape[1:]
    copies[0].wait()
    pack_pressure(p, both_x, both_y)
    copies[1].wait()
    pack_columns(v, (nj - 1, 0), (both_y.at[0, 2], both_y.at[1, 2]))
    copies[2].wait()
    both_x[0, 2] = u[:, ni - 1, :]
    both_x[1, 2] = u[:, 0, :]
    hx.write(mx, both_x, lax.axis_index("gx") % 2 == 0)
    hy.write(my, both_y, lax.axis_index("gy") % 2 == 0)
    for copy in copies[3:]:
        copy.wait()


def factor_kernel(groups, c, surface, lid, inv, mul, g0, gl, planes):
    depth, ni, nj = c.shape
    last, half = depth - 1, depth // 2
    group = lax.axis_index("lev")
    bottom = group == 0
    top = group == groups - 1
    ground = surface[...] - group * depth
    lidf = jnp.where(top, lid[...].astype(F32), 0.0)

    def coupling(k):
        return jnp.where(ground <= k - 1, c[k], 0.0)

    def diag(k):
        low = c[k] if k > 0 else jnp.where(bottom, c[k], 0.0)
        high = c[k + 1] if k < last else lidf * c[k]
        return 1.0 + low + high

    lo, hi = None, None
    for s in range(half):
        k, j = s, last - s
        d_lo, d_hi = diag(k), diag(j)
        if s:
            e_lo = coupling(k)
            m_lo = e_lo * lo
            mul[k] = m_lo
            d_lo = d_lo - e_lo * m_lo
            e_hi = coupling(j + 1)
            m_hi = e_hi * hi
            mul[j + 1] = m_hi
            d_hi = d_hi - e_hi * m_hi
        if j == half:
            e_mid = coupling(half)
            lo = jnp.where(ground <= k, 1.0 / d_lo, 0.0)
            m_mid = e_mid * lo
            mul[half] = m_mid
            d_hi = d_hi - e_mid * m_mid
        else:
            lo = jnp.where(ground <= k, 1.0 / d_lo, 0.0)
        hi = jnp.where(ground <= j, 1.0 / d_hi, 0.0)
        inv[k] = lo
        inv[j] = hi
    one = jnp.ones((ni, nj), F32)
    t0 = [one] + [None] * (half - 1)
    tl = [one] + [None] * (half - 1)
    for s in range(1, half):
        t0[s] = mul[s] * t0[s - 1]
        tl[s] = mul[last - s + 1] * tl[s - 1]
        g0[s] = t0[s]
        gl[last - s] = tl[s]
    g0[0] = one
    gl[last] = one
    xh0 = inv[half] * (mul[half] * t0[half - 1])
    xhl = inv[half] * tl[half - 1]
    xk0 = inv[half - 1] * t0[half - 1] + mul[half] * xh0
    xkl = mul[half] * xhl
    g0[half], gl[half] = xh0, xhl
    g0[half - 1], gl[half - 1] = xk0, xkl
    for s in range(1, half):
        k, j = half - 1 - s, half + s
        xk0 = inv[k] * g0[k] + mul[k + 1] * xk0
        xkl = mul[k + 1] * xkl
        xh0 = mul[j] * xh0
        xhl = inv[j] * gl[j] + mul[j] * xhl
        g0[k], gl[k] = xk0, xkl
        g0[j], gl[j] = xh0, xhl
    planes[0] = g0[0]
    planes[1] = g0[last]
    planes[2] = gl[last]
    planes[3] = c[0]


def condense(group, own, mate, cf):
    lower = group < 2
    is_inner = (group == 1) | (group == 2)
    inner = [jnp.where(is_inner, own[n], mate[n]) for n in range(4)]
    outer = [jnp.where(is_inner, mate[n], own[n]) for n in range(4)]
    x = inner[1]
    g_out, g_in = jnp.where(lower, outer[2], outer[0]), jnp.where(lower, inner[0], inner[2])
    c = jnp.where(lower, inner[3], outer[3])
    kappa = c / (1.0 + c * (g_out + g_in))
    cf[0] = kappa
    cf[1] = jnp.where(lower, inner[2], inner[0]) - kappa * x * x
    cf[2] = jnp.zeros_like(x)
    cf[3] = jnp.zeros_like(x)
    cf[4] = x
    cf[5] = g_out
    cf[6] = g_in
    cf[7] = inner[3]


def spread_setup(groups, group, own, got, st):
    st[group] = own[...]
    for m in range(1, groups):
        st[source_of(group, m, groups)] = got[m - 1][...]


def lane_matrix(nj):
    src = lax.broadcasted_iota(jnp.int32, (2 * nj, nj), 0) % nj
    dst = lax.broadcasted_iota(jnp.int32, (2 * nj, nj), 1)
    return jnp.where(src == dst + 1, 1.0, jnp.where(src == dst - 1, -1.0, 0.0)).astype(jnp.bfloat16)


def lane_difference(x, matrix):
    high = x.astype(jnp.bfloat16)
    low = (x - high.astype(F32)).astype(jnp.bfloat16)
    return jnp.dot(jnp.concatenate([high, low], 1), matrix, preferred_element_type=F32)


def add_rows(ref, rows):
    for r, plane in rows:
        ref[:, r, :] = ref[:, r, :] + plane


def interior_kernel(first, *refs):
    refs = list(refs)
    take = lambda n: [refs.pop(0) for _ in range(n)]
    zonal, merid, press = take(3)
    if first:
        vert = take(1)[0]
    else:
        uc, vc = take(2)
    zonal_out, merid_out, part = take(3)
    if first:
        copy = pltpu.make_async_copy(vert, take(1)[0], refs.pop())
        copy.start()
    pe, ue, square = take(3)
    depth, ni, nj = press.shape
    per = nj // ni
    rows = per * ni
    matrix = lane_matrix(nj)
    edge = jnp.zeros((depth, nj), F32)
    for ref in (pe, ue):
        ref[:, PAD - 1, :] = edge
        ref[:, PAD + ni, :] = edge
    above, below = slice(PAD + 1, PAD + 1 + ni), slice(PAD - 1, PAD - 1 + ni)
    if not first:
        square[...] = jnp.zeros(square.shape, F32)
    for b in range(depth // per):
        here = slice(b * per, (b + 1) * per)
        pe[here, PAD : PAD + ni, :] = press[here]
        zonal_out[here] = zonal[here] - H_STEP * (pe[here, above, :] - pe[here, below, :])
    if not first:
        add_rows(zonal_out, ((0, uc[0]), (ni - 1, uc[1])))
    for b in range(depth // per):
        here = slice(b * per, (b + 1) * per)
        p = press[here].reshape(rows, nj)
        ue[here, PAD : PAD + ni, :] = zonal_out[here]
        v = merid[here].reshape(rows, nj)
        if not first:
            square[0:1, :] = vc[0, b : b + 1, :]
            square[nj - 1 : nj, :] = vc[1, b : b + 1, :]
            v = v + square[...].T
        v = v - H_STEP * lane_difference(p, matrix)
        merid_out[here] = v.reshape(per, ni, nj)
        spread = (ue[here, above, :] - ue[here, below, :]).reshape(rows, nj) + lane_difference(v, matrix)
        part[here] = (p - D_STEP * spread).reshape(per, ni, nj)
    if first:
        copy.wait()


def emit_kernel(zonal, merid, uc, vc, zonal_out, merid_out, square):
    depth, ni, nj = zonal.shape
    per = nj // ni
    square[...] = jnp.zeros(square.shape, F32)
    for b in range(depth // per):
        here = slice(b * per, (b + 1) * per)
        square[0:1, :] = vc[0, b : b + 1, :]
        square[nj - 1 : nj, :] = vc[1, b : b + 1, :]
        merid_out[here] = merid[here] + square[...].T.reshape(per, ni, nj)
        zonal_out[here] = zonal[here]
    add_rows(zonal_out, ((0, uc[0]), (ni - 1, uc[1])))


def solve_kernel(first, final, hx, hy, groups, *refs):
    refs = list(refs)
    take = lambda n: [refs.pop(0) for _ in range(n)]
    paired = groups == 4
    part0, vert, inv, mul = take(4)
    ox, oy = take(hx.count), take(hy.count)
    rx, ry = take(hx.count), take(hy.count)
    uh, vh = (None, None) if first else take(2)
    if paired:
        own_s, mate_s = take(2) if first else (None, None)
        cf = None if first else take(1)[0]
    y_out, part, planes, uc, vc = take(5)
    across = take(2) if paired else None
    if paired and first:
        cf = take(1)[0]
    uh_out, vh_out = (None, None) if final else take(2)
    square = take(1)[0]
    depth, ni, nj = part0.shape
    last, half, per = depth - 1, depth // 2, nj // ni
    group = lax.axis_index("lev")
    even_x, even_y = lax.axis_index("gx") % 2 == 0, lax.axis_index("gy") % 2 == 0
    if paired and first:
        condense(group, own_s, mate_s, cf)

    u_lo = hx.low(rx, 2, even_x) if first else uh[0]
    u_hi = hx.high(rx, 2, even_x) if first else uh[1]
    u_lo = u_lo - H_STEP * (hx.down(ox, 0, even_x) - hx.low(rx, 0, even_x))
    u_hi = u_hi - H_STEP * (hx.high(rx, 1, even_x) - hx.up(ox, 1, even_x))
    u_first, u_last = H_STEP * hx.low(rx, 1, even_x), -H_STEP * hx.high(rx, 0, even_x)
    uc[0], uc[1] = u_first, u_last
    v_lo = hy.low(ry, 2, even_y) if first else vh[0]
    v_hi = hy.high(ry, 2, even_y) if first else vh[1]
    v_lo = v_lo - H_STEP * (hy.down(oy, 0, even_y) - hy.low(ry, 0, even_y))
    v_hi = v_hi - H_STEP * (hy.high(ry, 1, even_y) - hy.up(oy, 1, even_y))
    if not final:
        uh_out[0], uh_out[1] = u_lo, u_hi
        vh_out[0], vh_out[1] = v_lo, v_hi
    v_first, v_last = H_STEP * hy.low(ry, 1, even_y), -H_STEP * hy.high(ry, 0, even_y)
    vc[0], vc[1] = v_first, v_last
    square[...] = jnp.zeros(square.shape, F32)
    for b in range(depth // per):
        here = slice(b * per, (b + 1) * per)
        one = slice(b, b + 1)
        square[0:1, :] = D_STEP * v_lo[one]
        square[1:2, :] = D_STEP * v_first[one]
        square[nj - 2 : nj - 1, :] = -D_STEP * v_last[one]
        square[nj - 1 : nj, :] = -D_STEP * v_hi[one]
        part[here] = part0[here] + square[...].T.reshape(per, ni, nj)
    edges = ((0, D_STEP * u_lo), (1, D_STEP * u_first), (ni - 2, -D_STEP * u_last), (ni - 1, -D_STEP * u_hi))
    add_rows(part, edges)

    lo = vert[0] - V_STEP * part[1]
    hi = vert[last] + V_STEP * part[last - 1]
    y_out[0], y_out[last] = lo, hi
    for s in range(1, half):
        k, j = s, last - s
        lo = (vert[k] - V_STEP * (part[k + 1] - part[k - 1])) + mul[k] * lo
        hi = (vert[j] - V_STEP * (part[j + 1] - part[j - 1])) + mul[j + 1] * hi
        y_out[k], y_out[j] = lo, hi
    hi = inv[half] * (hi + mul[half] * lo)
    lo = inv[half - 1] * lo + mul[half] * hi
    y_out[half], y_out[half - 1] = hi, lo
    for s in range(1, half):
        k, j = half - 1 - s, half + s
        lo = inv[k] * y_out[k] + mul[k + 1] * lo
        hi = inv[j] * y_out[j] + mul[j] * hi
        y_out[k], y_out[j] = lo, hi
    p_first, p_last = part[0], part[last]
    planes[0], planes[1] = lo, hi
    planes[2], planes[3] = p_first, p_last
    if paired:
        lower = group < 2
        sign = jnp.where(lower, V_STEP, -V_STEP)
        y_near, y_far = jnp.where(lower, hi, lo), jnp.where(lower, lo, hi)
        p_near, p_far = jnp.where(lower, p_last, p_first), jnp.where(lower, p_first, p_last)
        gain = cf[4] * cf[0]
        inside = y_near - gain * (cf[5] * (sign * p_far) + y_far)
        outside = cf[4] * (sign * p_near) + gain * (y_near - cf[6] * (sign * p_near))
        inside = jnp.where((group == 1) | (group == 2), inside, outside)
        for message in across:
            message[0], message[1] = inside, p_near
        if first:
            across[0][2], across[0][3] = cf[1], cf[7]


def paired_sources(group, cf, own, mate, crossed, lv):
    lower = group < 2
    is_inner = (group == 1) | (group == 2)
    sign = jnp.where(lower, V_STEP, -V_STEP)
    near = jnp.where(lower, 1, 0)
    slot = jnp.where(is_inner, 0, 1)
    lv[slot] = own[...]
    lv[1 - slot] = mate[...]
    kappa, mine, other, gain, x, g_out, g_in = (cf[n] for n in range(7))
    y_in_near, y_in_far, y_out = lv[0, near], lv[0, 1 - near], lv[1, near]
    p_in_near = sign * lv[0, 2 + near]
    p_in_far = sign * lv[0, 3 - near]
    p_out = sign * lv[1, 2 + near]
    flux = kappa * ((y_out - g_out * p_in_far) - (y_in_far + g_in * p_out))
    here = y_in_near + x * (p_out + flux)
    there = crossed[0][0] + crossed[1][0]
    p_there = sign * jnp.where(is_inner, crossed[1][1], crossed[0][1])
    middle = gain * ((there - here) + (other * p_in_near + mine * p_there))
    n_here = middle - p_there
    n_there = p_in_near - middle
    flux = flux - kappa * x * n_here
    in_far = p_out + flux
    out_near = -(p_in_far + flux)
    near_source = jnp.where(is_inner, n_here, out_near)
    far_source = jnp.where(is_inner, in_far, 0.0)
    alpha = jnp.where(lower, far_source, near_source)
    beta = jnp.where(lower, near_source, far_source)
    under = jnp.where(
        group == 1,
        y_out + g_out * out_near,
        jnp.where(
            group == 2,
            there + other * n_there,
            jnp.where(group == 3, y_in_far + g_in * in_far + x * n_here, 0.0),
        ),
    )
    return alpha, beta, under


def chain_sources(groups, group, st, own, got, lv):
    lv[group] = own[...]
    for m in range(1, groups):
        lv[source_of(group, m, groups)] = got[m - 1][...]
    zero = jnp.zeros(own.shape[1:], F32)
    z_top, z_bot = [], []
    for g in range(groups):
        below = V_STEP * lv[g - 1, 3] if g else zero
        above = V_STEP * lv[g + 1, 2] if g < groups - 1 else zero
        z_top.append(lv[g, 0] + st[g, 0] * below - st[g, 1] * above)
        z_bot.append(lv[g, 1] + st[g, 1] * below - st[g, 2] * above)
    ratios, parts = [zero], [zero]
    for g in range(1, groups):
        cg = st[g, 3]
        down = cg * st[g - 1, 1]
        pivot = 1.0 / (1.0 + cg * (st[g - 1, 2] + st[g, 0]) - down * ratios[-1])
        parts.append((cg * (z_bot[g - 1] - z_top[g]) + down * parts[-1]) * pivot)
        ratios.append(cg * st[g, 1] * pivot)
    flux = [zero] * (groups + 1)
    for g in range(groups - 1, 0, -1):
        flux[g] = parts[g] + ratios[g] * flux[g + 1]
    alpha, beta, under = zero, zero, zero
    for g in range(groups):
        mine = group == g
        if g:
            alpha = jnp.where(mine, V_STEP * lv[g - 1, 3] + flux[g], alpha)
            bot = z_bot[g - 1] + st[g - 1, 1] * flux[g - 1] - st[g - 1, 2] * flux[g]
            under = jnp.where(mine, bot, under)
        if g < groups - 1:
            beta = jnp.where(mine, -(V_STEP * lv[g + 1, 2] + flux[g + 1]), beta)
    return alpha, beta, under


def finish_kernel(groups, first, final, hx, hy, *refs):
    refs = list(refs)
    take = lambda n: [refs.pop(0) for _ in range(n)]
    y, part, g0, gl, own = take(5)
    got = take(groups - 1)
    paired = groups == 4
    system = take(1)[0]
    setups = take(groups) if first and not paired else ()
    vert_out, press_out = take(2)
    mx, my = ([], []) if final else (take(hx.count), take(hy.count))
    if first:
        early, system = system, take(1)[0]
    lv = take(1)[0]
    depth, _, _ = y.shape
    group = lax.axis_index("lev")
    if paired:
        if first:
            for n in (0, 1, 4, 5, 6):
                system[n] = early[n]
            other = got[1][2]
            c = jnp.where(group < 2, got[1][3], early[7])
            system[2] = other
            system[3] = c / (1.0 + c * (early[1] + other))
        alpha, beta, under = paired_sources(group, system, own, got[0], got[1:], lv)
    else:
        if first:
            spread_setup(groups, group, setups[0], setups[1:], system)
        alpha, beta, under = chain_sources(groups, group, system, own, got, lv)
    vert, press = take(2) if final else (vert_out, press_out)

    def level(k, w_prev):
        w = y[k] + g0[k] * alpha + gl[k] * beta
        vert[k] = w
        press[k] = part[k] - P_STEP * (w - w_prev)
        return w

    if final:
        sems = take(1)[0]
        step, w, copies = max(depth // 4, 1), under, []
        for start in range(0, depth, step):
            stop = min(start + step, depth)
            w = lax.fori_loop(start, stop, level, w, unroll=True)
            for n, (a, b) in enumerate(((vert, vert_out), (press, press_out))):
                here = pl.ds(start, stop - start)
                copies.append(pltpu.make_async_copy(a.at[here], b.at[here], sems.at[n, start // step]))
                copies[-1].start()
        for copy in copies:
            copy.wait()
        return
    lax.fori_loop(0, depth, level, under, unroll=4)
    both_x, both_y = take(2)
    pack_pressure(press_out, both_x, both_y)
    hx.write(mx, both_x, lax.axis_index("gx") % 2 == 0)
    hy.write(my, both_y, lax.axis_index("gy") % 2 == 0)


def body(zonal, meridional, vertical, pressure, coupling, surface, lid_flag):
    depth, ni, nj = coupling.shape
    full, four, two = (depth, ni, nj), (4, ni, nj), (2, ni, nj)
    groups = lax.axis_size("lev")
    hx = Halo("gx", (depth, nj))
    hy = Halo("gy", (depth // (nj // ni), nj))
    wide = pltpu.VMEM((depth, ni + 2 * PAD, nj), F32)
    square = pltpu.VMEM((nj, nj), F32)

    inputs = (pressure, meridional, zonal, coupling, surface, lid_flag)
    results = call(
        functools.partial(first_kernel, hx, hy),
        [full] * 4 + [surface.shape] * 2 + hx.shapes(3) + hy.shapes(3),
        [pltpu.with_memory_space_constraint(a, pltpu.HBM) for a in inputs],
        scratch=[hx.scratch(3), hy.scratch(3), pltpu.SemaphoreType.DMA((6,))],
        spaces=[HBM] * 6,
        types=[a.dtype for a in inputs],
    )
    pressure, meridional, zonal, coupling, surface, lid_flag = results[:6]
    ox, oy = results[6 : 6 + hx.count], results[6 + hx.count :]
    ry, rx = hy.exchange(oy), hx.exchange(ox)
    inv, mul, g0, gl, own_s = call(
        functools.partial(factor_kernel, groups), [full] * 4 + [four], [coupling, surface, lid_flag]
    )
    paired = groups == 4
    got_s = [to_lev(own_s, m) for m in range(1, 2 if paired else groups)]
    setup = (8 if paired else 4 * groups, ni, nj)
    system = uh = vh = uc = vc = None
    for substep in range(SUBSTEPS):
        first, final = substep == 0, substep == SUBSTEPS - 1
        args = [zonal, meridional, pressure]
        args += [pltpu.with_memory_space_constraint(vertical, pltpu.HBM)] if first else [uc, vc]
        results = call(
            functools.partial(interior_kernel, first),
            [full] * (4 if first else 3),
            args,
            scratch=[wide, wide, square] + ([pltpu.SemaphoreType.DMA(())] if first else []),
            spaces=[VMEM] * 3 + [HBM] if first else None,
        )
        zonal, meridional, part = results[:3]
        if first:
            vertical = results[3]
        args = [part, vertical, inv, mul] + ox + oy + rx + ry
        args += [] if first else [uh, vh]
        if paired:
            args += [own_s] + got_s if first else [system]
        ends = [(2,) + hx.plane, (2,) + hy.plane]
        outs = [full, full, four] + ends
        if paired:
            outs += [four if first else two, two] + ([setup] if first else [])
        outs += [] if final else ends
        results = call(functools.partial(solve_kernel, first, final, hx, hy, groups), outs, args, scratch=[square])
        y, part, own, uc, vc = results[:5]
        if not final:
            uh, vh = results[-2:]
        if paired:
            got = [to_lev(a, m) for m, a in ((1, own), (2, results[5]), (3, results[6]))]
            if first:
                system = results[7]
        else:
            got = [to_lev(own, m) for m in range(1, groups)]
        if final:
            zonal, meridional = call(emit_kernel, [full] * 2, [zonal, meridional, uc, vc], scratch=[square])
        args = [y, part, g0, gl, own] + got + [own_s if system is None else system]
        if first and not paired:
            args += [own_s] + got_s
        outs, scratch = [full, full], [pltpu.VMEM((groups, 4, ni, nj), F32)]
        if not final:
            outs += hx.shapes(2) + hy.shapes(2)
        if first:
            outs += [setup if paired else (groups, 4, ni, nj)]
        if final:
            scratch += [pltpu.VMEM(full, F32)] * 2 + [pltpu.SemaphoreType.DMA((2, 4))]
        else:
            scratch += [hx.scratch(2), hy.scratch(2)]
        results = call(
            functools.partial(finish_kernel, groups, first, final, hx, hy),
            outs,
            args,
            scratch=scratch,
            out_spaces=[HBM] * 2 if final else None,
        )
        vertical, pressure = results[:2]
        if first:
            system = results[-1]
        if not final:
            ox, oy = results[2 : 2 + hx.count], results[2 + hx.count : 2 + hx.count + hy.count]
            ry, rx = hy.exchange(oy), hx.exchange(ox)
    return (zonal, meridional, vertical, pressure)


def solution(mesh):
    block = P("lev", "gx", "gy")
    plane = P("gx", "gy")

    return jax.shard_map(
        body,
        mesh=mesh,
        in_specs=(block,) * 5 + (plane,) * 2,
        out_specs=(block,) * 4,
        check_vma=False,
    )
```

profile of v0, /device:TPU:0, one launch (start us, length us, event | category | flops | bytes accessed | tf_op | source)
XLA Modules:
  0.0 43.7 jit_solution(8936596132026874709)
XLA Ops:
  0.6 1.6 %shard_map.102 = (f32[32,32,128]{2,1,0:T(8,128)S(1)}, f32[32,32,128]{2,1,0:T(8,128)S(1)}, f32[32,32,128]{2,1,0:T(8,128)S(1)}, f32[32,32,128]{2,1,0:T(8,128)S(1)}...) custom-call(f32[32,32,128]{2,1,0:T(8,128)} %refs_0_.1, ...), custom_call_target="tpu_custom_call" | custom-call | tf_op jit(solution)/shard_map/pallas_call | solution.py:24
  2.2 3.0 %collective-permute-start = (f32[6,32,128]{2,1,0:T(8,128)S(1)}, f32[6,32,128]{2,1,0:T(8,128)S(1)}, u32[]{:S(2)}, u32[]{:S(2)}) collective-permute-start(f32[6,32,128]{2,1,0:T(8,128)S(1)} %get-tuple-element.81.refs_4_), channel_id=1, source_target_pairs={{0,16},{16,0},{1,17},{17,1},{2,18},{18,2},{3,19},{19,3},{4,20},{20... | collective-permute-start | bytes 294920 | tf_op jit(solution)/shard_map/ppermute | solution.py:91
  5.2 0.3 shard_map.104
  5.5 0.1 collective-permute-start.3
  5.6 1.6 %collective-permute-start.1 = (f32[3,8,128]{2,1,0:T(8,128)S(1)}, f32[3,8,128]{2,1,0:T(8,128)S(1)}, u32[]{:S(2)}, u32[]{:S(2)}) collective-permute-start(f32[3,8,128]{2,1,0:T(8,128)S(1)} %get-tuple-element.82.refs_5_), channel_id=1, source_target_pairs={{0,4},{4,0},{8,12},{12,8},{1,5},{5,1},{9,13},{13,9},{2,6},{6,2},{1... | collective-permute-start | bytes 36872 | tf_op jit(solution)/shard_map/ppermute | solution.py:88
  7.3 2.5 %collective-permute-start.2 = (f32[3,8,128]{2,1,0:T(8,128)S(1)}, f32[3,8,128]{2,1,0:T(8,128)S(1)}, u32[]{:S(2)}, u32[]{:S(2)}) collective-permute-start(f32[3,8,128]{2,1,0:T(8,128)S(1)} %get-tuple-element.83.refs_6_), channel_id=1, source_target_pairs={{0,12},{4,8},{8,4},{12,0},{1,13},{5,9},{9,5},{13,1},{2,14},{6,10},... | collective-permute-start | bytes 36872 | tf_op jit(solution)/shard_map/ppermute | solution.py:87
  9.7 1.1 %shard_map.103 = (f32[32,32,128]{2,1,0:T(8,128)S(1)}, f32[32,32,128]{2,1,0:T(8,128)S(1)}, f32[32,32,128]{2,1,0:T(8,128)S(1)}, f32[32,32,128]{2,1,0:T(8,128)S(1)}) custom-call(f32[32,32,128]{2,1,0:T(8,128)S(1)} %get-tuple-element.69.refs_0_, f32[32,32,128]{2,1,0:T(8,128)S(1)} %get-tuple-element.70.refs_1_, f32[32,32,128]{2,1,0:T(8,128)S(1)} %get-tuple-element.71.refs_2_, ...), custom_call_target="tpu_custom_call" | custom-call | tf_op jit(solution)/shard_map/pallas_call | solution.py:24
  10.8 0.0 collective-permute-done.1.refs_8_
  10.8 1.9 %collective-permute-done.2.refs_9_ = f32[3,8,128]{2,1,0:T(8,128)S(1)} collective-permute-done((f32[3,8,128]{2,1,0:T(8,128)S(1)}, f32[3,8,128]{2,1,0:T(8,128)S(1)}, u32[]{:S(2)}, u32[]{:S(2)}) %collective-permute-start.2) | collective-permute-done | bytes 12320 | tf_op jit(solution)/shard_map/ppermute | solution.py:87
  12.7 0.0 collective-permute-done.3.refs_11_
  12.8 0.0 collective-permute-done.refs_7_
  12.8 0.5 %shard_map.105 = (f32[32,32,128]{2,1,0:T(8,128)S(1)}, f32[32,32,128]{2,1,0:T(8,128)S(1)}, f32[4,32,128]{2,1,0:T(8,128)S(1)}, f32[2,32,128]{2,1,0:T(8,128)S(1)}, ...) custom-call(f32[32,32,128]{2,1,0:T(8,128)S(1)} %get-tuple-element.74, ...), custom_call_target="tpu_custom_call" | custom-call | tf_op jit(solution)/shard_map/pallas_call | solution.py:24
  13.2 1.6 %collective-permute-start.5 = (f32[4,32,128]{2,1,0:T(8,128)S(1)}, f32[4,32,128]{2,1,0:T(8,128)S(1)}, u32[]{:S(2)}, u32[]{:S(2)}) collective-permute-start(f32[4,32,128]{2,1,0:T(8,128)S(1)} %get-tuple-element.90), channel_id=1, source_target_pairs={{0,2},{1,3},{2,0},{3,1},{4,6},{5,7},{6,4},{7,5},{8,10},{9,11},{10,... | collective-permute-start | bytes 196616 | tf_op jit(solution)/shard_map/ppermute | solution.py:99
  14.8 0.0 collective-permute-start.4
  14.8 0.6 %collective-permute-start.6 = (f32[2,32,128]{2,1,0:T(8,128)S(1)}, f32[2,32,128]{2,1,0:T(8,128)S(1)}, u32[]{:S(2)}, u32[]{:S(2)}) collective-permute-start(f32[2,32,128]{2,1,0:T(8,128)S(1)} %get-tuple-element.91), channel_id=1, source_target_pairs={{0,3},{1,2},{2,1},{3,0},{4,7},{5,6},{6,5},{7,4},{8,11},{9,10},{10,... | collective-permute-start | bytes 98312 | tf_op jit(solution)/shard_map/ppermute | solution.py:99
  15.5 2.7 %collective-permute-done.6.refs_7_ = f32[2,32,128]{2,1,0:T(8,128)S(1)} collective-permute-done((f32[2,32,128]{2,1,0:T(8,128)S(1)}, f32[2,32,128]{2,1,0:T(8,128)S(1)}, u32[]{:S(2)}, u32[]{:S(2)}) %collective-permute-start.6) | collective-permute-done | bytes 32800 | tf_op jit(solution)/shard_map/ppermute | solution.py:99
  18.2 0.0 collective-permute-done.5.refs_6_
  18.2 0.0 collective-permute-done.4.refs_5_
  18.2 0.4 %shard_map.106 = (f32[32,32,128]{2,1,0:T(8,128)S(1)}, f32[32,32,128]{2,1,0:T(8,128)S(1)}, f32[4,32,128]{2,1,0:T(8,128)S(1)}, f32[2,8,128]{2,1,0:T(8,128)S(1)}, f...) custom-call(f32[32,32,128]{2,1,0:T(8,128)S(1)} %get-tuple-element.85.refs_0_, ...), custom_call_target="tpu_custom_call" | custom-call | tf_op jit(solution)/shard_map/pallas_call | solution.py:24
  18.6 0.6 %collective-permute-start.7 = (f32[4,32,128]{2,1,0:T(8,128)S(1)}, f32[4,32,128]{2,1,0:T(8,128)S(1)}, u32[]{:S(2)}, u32[]{:S(2)}) collective-permute-start(f32[4,32,128]{2,1,0:T(8,128)S(1)} %get-tuple-element.100.refs_4_), channel_id=1, source_target_pairs={{0,16},{16,0},{1,17},{17,1},{2,18},{18,2},{3,19},{19,3},{4,20},{20... | collective-permute-start | bytes 196616 | tf_op jit(solution)/shard_map/ppermute | solution.py:91
  19.2 2.5 %collective-permute-start.9 = (f32[2,8,128]{2,1,0:T(8,128)S(1)}, f32[2,8,128]{2,1,0:T(8,128)S(1)}, u32[]{:S(2)}, u32[]{:S(2)}) collective-permute-start(f32[2,8,128]{2,1,0:T(8,128)S(1)} %get-tuple-element.102.refs_6_), channel_id=1, source_target_pairs={{0,12},{4,8},{8,4},{12,0},{1,13},{5,9},{9,5},{13,1},{2,14},{6,10},... | collective-permute-start | bytes 24584 | tf_op jit(solution)/shard_map/ppermute | solution.py:87
  21.7 0.7 %shard_map.107 = (f32[32,32,128]{2,1,0:T(8,128)S(1)}, f32[32,32,128]{2,1,0:T(8,128)S(1)}, f32[32,32,128]{2,1,0:T(8,128)S(1)}) custom-call(f32[32,32,128]{2,1,0:T(8,128)S(1)} %get-tuple-element.72.refs_0_, f32[32,32,128]{2,1,0:T(8,128)S(1)} %get-tuple-element.73.refs_1_, f32[32,32,128]{2,1,0:T(8,128)S(1)} %get-tuple-element.93.refs_2_, ...), custom_call_target="tpu_custom_call" | custom-call | tf_op jit(solution)/shard_map/pallas_call | solution.py:24
  22.4 0.5 %collective-permute-done.8.refs_8_ = f32[2,8,128]{2,1,0:T(8,128)S(1)} collective-permute-done((f32[2,8,128]{2,1,0:T(8,128)S(1)}, f32[2,8,128]{2,1,0:T(8,128)S(1)}, u32[]{:S(2)}, u32[]{:S(2)}) %collective-permute-start.8) | collective-permute-done | bytes 8224 | tf_op jit(solution)/shard_map/ppermute | solution.py:88
  22.9 1.8 %collective-permute-done.9.refs_9_ = f32[2,8,128]{2,1,0:T(8,128)S(1)} collective-permute-done((f32[2,8,128]{2,1,0:T(8,128)S(1)}, f32[2,8,128]{2,1,0:T(8,128)S(1)}, u32[]{:S(2)}, u32[]{:S(2)}) %collective-permute-start.9) | collective-permute-done | bytes 8224 | tf_op jit(solution)/shard_map/ppermute | solution.py:87
  24.7 0.0 collective-permute-done.7.refs_7_
  24.7 0.5 %shard_map.108 = (f32[32,32,128]{2,1,0:T(8,128)S(1)}, f32[32,32,128]{2,1,0:T(8,128)S(1)}, f32[4,32,128]{2,1,0:T(8,128)S(1)}, f32[2,32,128]{2,1,0:T(8,128)S(1)}, ...) custom-call(f32[32,32,128]{2,1,0:T(8,128)S(1)} %get-tuple-element.98, ...), custom_call_target="tpu_custom_call" | custom-call | tf_op jit(solution)/shard_map/pallas_call | solution.py:24
  25.2 0.1 collective-permute-start.10
  25.2 1.3 %collective-permute-start.11 = (f32[2,32,128]{2,1,0:T(8,128)S(1)}, f32[2,32,128]{2,1,0:T(8,128)S(1)}, u32[]{:S(2)}, u32[]{:S(2)}) collective-permute-start(f32[2,32,128]{2,1,0:T(8,128)S(1)} %get-tuple-element.109), channel_id=1, source_target_pairs={{0,2},{1,3},{2,0},{3,1},{4,6},{5,7},{6,4},{7,5},{8,10},{9,11},{10,... | collective-permute-start | bytes 98312 | tf_op jit(solution)/shard_map/ppermute | solution.py:99
  26.5 0.6 %collective-permute-start.12 = (f32[2,32,128]{2,1,0:T(8,128)S(1)}, f32[2,32,128]{2,1,0:T(8,128)S(1)}, u32[]{:S(2)}, u32[]{:S(2)}) collective-permute-start(f32[2,32,128]{2,1,0:T(8,128)S(1)} %get-tuple-element.110), channel_id=1, source_target_pairs={{0,3},{1,2},{2,1},{3,0},{4,7},{5,6},{6,5},{7,4},{8,11},{9,10},{10,... | collective-permute-start | bytes 98312 | tf_op jit(solution)/shard_map/ppermute | solution.py:99
  27.1 2.1 %collective-permute-done.11.refs_6_ = f32[2,32,128]{2,1,0:T(8,128)S(1)} collective-permute-done((f32[2,32,128]{2,1,0:T(8,128)S(1)}, f32[2,32,128]{2,1,0:T(8,128)S(1)}, u32[]{:S(2)}, u32[]{:S(2)}) %collective-permute-start.11) | collective-permute-done | bytes 32800 | tf_op jit(solution)/shard_map/ppermute | solution.py:99
  29.2 0.6 %collective-permute-done.12.refs_7_ = f32[2,32,128]{2,1,0:T(8,128)S(1)} collective-permute-done((f32[2,32,128]{2,1,0:T(8,128)S(1)}, f32[2,32,128]{2,1,0:T(8,128)S(1)}, u32[]{:S(2)}, u32[]{:S(2)}) %collective-permute-start.12) | collective-permute-done | bytes 32800 | tf_op jit(solution)/shard_map/ppermute | solution.py:99
  29.9 0.0 collective-permute-done.10.refs_5_
  29.9 0.4 %shard_map.109 = (f32[32,32,128]{2,1,0:T(8,128)S(1)}, f32[32,32,128]{2,1,0:T(8,128)S(1)}, f32[4,32,128]{2,1,0:T(8,128)S(1)}, f32[2,8,128]{2,1,0:T(8,128)S(1)}, f32[2,8,128]{2,1,0:T(8,128)S(1)}) custom-call(f32[32,32,128]{2,1,0:T(8,128)S(1)} %get-tuple-element.106.refs_0_, f32[32,32,128]{2,1,0:T(8,128)S(1)} %get-tuple-element.107.refs_1_, ...), custom_call_target="tpu_custom_call" | custom-call | tf_op jit(solution)/shard_map/pallas_call | solution.py:24
  30.3 1.6 %collective-permute-start.13 = (f32[4,32,128]{2,1,0:T(8,128)S(1)}, f32[4,32,128]{2,1,0:T(8,128)S(1)}, u32[]{:S(2)}, u32[]{:S(2)}) collective-permute-start(f32[4,32,128]{2,1,0:T(8,128)S(1)} %get-tuple-element.118.refs_4_), channel_id=1, source_target_pairs={{0,16},{16,0},{1,17},{17,1},{2,18},{18,2},{3,19},{19,3},{4,20},{20... | collective-permute-start | bytes 196616 | tf_op jit(solution)/shard_map/ppermute | solution.py:91
  31.9 0.2 collective-permute-start.14
  32.1 2.5 %collective-permute-start.15 = (f32[2,8,128]{2,1,0:T(8,128)S(1)}, f32[2,8,128]{2,1,0:T(8,128)S(1)}, u32[]{:S(2)}, u32[]{:S(2)}) collective-permute-start(f32[2,8,128]{2,1,0:T(8,128)S(1)} %get-tuple-element.120.refs_6_), channel_id=1, source_target_pairs={{0,12},{4,8},{8,4},{12,0},{1,13},{5,9},{9,5},{13,1},{2,14},{6,10},... | collective-permute-start | bytes 24584 | tf_op jit(solution)/shard_map/ppermute | solution.py:87
  34.6 0.7 %shard_map.110 = (f32[32,32,128]{2,1,0:T(8,128)S(1)}, f32[32,32,128]{2,1,0:T(8,128)S(1)}, f32[32,32,128]{2,1,0:T(8,128)S(1)}) custom-call(f32[32,32,128]{2,1,0:T(8,128)S(1)} %get-tuple-element.96.refs_0_, f32[32,32,128]{2,1,0:T(8,128)S(1)} %get-tuple-element.97.refs_1_, f32[32,32,128]{2,1,0:T(8,128)S(1)} %get-tuple-element.111.refs_2_, ...), custom_call_target="tpu_custom_call" | custom-call | tf_op jit(solution)/shard_map/pallas_call | solution.py:24
  35.3 0.3 collective-permute-done.14.refs_8_
  35.5 2.0 %collective-permute-done.15.refs_9_ = f32[2,8,128]{2,1,0:T(8,128)S(1)} collective-permute-done((f32[2,8,128]{2,1,0:T(8,128)S(1)}, f32[2,8,128]{2,1,0:T(8,128)S(1)}, u32[]{:S(2)}, u32[]{:S(2)}) %collective-permute-start.15) | collective-permute-done | bytes 8224 | tf_op jit(solution)/shard_map/ppermute | solution.py:87
  37.5 0.5 %shard_map.111 = (f32[32,32,128]{2,1,0:T(8,128)S(1)}, f32[32,32,128]{2,1,0:T(8,128)S(1)}, f32[4,32,128]{2,1,0:T(8,128)S(1)}, f32[2,32,128]{2,1,0:T(8,128)S(1)}, ...) custom-call(f32[32,32,128]{2,1,0:T(8,128)S(1)} %get-tuple-element.116.refs_0_, ...), custom_call_target="tpu_custom_call" | custom-call | tf_op jit(solution)/shard_map/pallas_call | solution.py:24
  38.0 0.1 collective-permute-start.16
  38.1 1.1 %collective-permute-start.17 = (f32[2,32,128]{2,1,0:T(8,128)S(1)}, f32[2,32,128]{2,1,0:T(8,128)S(1)}, u32[]{:S(2)}, u32[]{:S(2)}) collective-permute-start(f32[2,32,128]{2,1,0:T(8,128)S(1)} %get-tuple-element.130), channel_id=1, source_target_pairs={{0,2},{1,3},{2,0},{3,1},{4,6},{5,7},{6,4},{7,5},{8,10},{9,11},{10,... | collective-permute-start | bytes 98312 | tf_op jit(solution)/shard_map/ppermute | solution.py:99
  39.2 0.8 %collective-permute-start.18 = (f32[2,32,128]{2,1,0:T(8,128)S(1)}, f32[2,32,128]{2,1,0:T(8,128)S(1)}, u32[]{:S(2)}, u32[]{:S(2)}) collective-permute-start(f32[2,32,128]{2,1,0:T(8,128)S(1)} %get-tuple-element.131), channel_id=1, source_target_pairs={{0,3},{1,2},{2,1},{3,0},{4,7},{5,6},{6,5},{7,4},{8,11},{9,10},{10,... | collective-permute-start | bytes 98312 | tf_op jit(solution)/shard_map/ppermute | solution.py:99
  39.9 1.2 %shard_map.112 = (f32[32,32,128]{2,1,0:T(8,128)}, f32[32,32,128]{2,1,0:T(8,128)}) custom-call(f32[32,32,128]{2,1,0:T(8,128)S(1)} %get-tuple-element.114.zonal, f32[32,32,128]{2,1,0:T(8,128)S(1)} %get-tuple-element.115.merid, f32[2,32,128]{2,1,0:T(8,128)S(1)} %get-tuple-element.123.uc, f32[2,8,128]{2,1,0:T(8,128)S(1)} %get-tuple-element.124.vc), custom_call_target="tpu_custom_call" | custom-call | tf_op jit(solution)/shard_map/pallas_call | solution.py:24
  41.1 0.9 %collective-permute-done.17.refs_6_ = f32[2,32,128]{2,1,0:T(8,128)S(1)} collective-permute-done((f32[2,32,128]{2,1,0:T(8,128)S(1)}, f32[2,32,128]{2,1,0:T(8,128)S(1)}, u32[]{:S(2)}, u32[]{:S(2)}) %collective-permute-start.17) | collective-permute-done | bytes 32800 | tf_op jit(solution)/shard_map/ppermute | solution.py:99
  42.1 0.5 %collective-permute-done.18.refs_7_ = f32[2,32,128]{2,1,0:T(8,128)S(1)} collective-permute-done((f32[2,32,128]{2,1,0:T(8,128)S(1)}, f32[2,32,128]{2,1,0:T(8,128)S(1)}, u32[]{:S(2)}, u32[]{:S(2)}) %collective-permute-start.18) | collective-permute-done | bytes 32800 | tf_op jit(solution)/shard_map/ppermute | solution.py:99
  42.5 0.0 collective-permute-done.16.refs_5_
  42.5 1.1 %shard_map.113 = (f32[32,32,128]{2,1,0:T(8,128)}, f32[32,32,128]{2,1,0:T(8,128)}) custom-call(f32[32,32,128]{2,1,0:T(8,128)S(1)} %get-tuple-element.127.refs_0_, f32[32,32,128]{2,1,0:T(8,128)S(1)} %get-tuple-element.128.refs_1_, f32[32,32,128]{2,1,0:T(8,128)S(1)} %get-tuple-element.87.refs_2_, f32[32,32,128]{2,1,0:T(8,128)S(1)} %get-tuple-element.88.refs_3_, ...), custom_call_target="tpu_custom_call" | custom-call | tf_op jit(solution)/shard_map/pallas_call | solution.py:24
  (2 shorter events, 0.0 us)
Async XLA Ops:
  2.2 10.5 %collective-permute-start = (f32[6,32,128]{2,1,0:T(8,128)S(1)}, f32[6,32,128]{2,1,0:T(8,128)S(1)}, u32[]{:S(2)}, u32[]{:S(2)}) collective-permute-start(f32[6,32,128]{2,1,0:T(8,128)S(1)} %get-tuple-element.81.refs_4_), channel_id=1, source_target_pairs={{0,16},{16,0},{1,17},{17,1},{2,18},{18,2},{3,19},{19,3},{4,20},{20... | collective-permute-start | bytes 294920 | tf_op jit(solution)/shard_map/ppermute | solution.py:91
  5.5 7.2 %collective-permute-start.3 = (f32[4,32,128]{2,1,0:T(8,128)S(1)}, f32[4,32,128]{2,1,0:T(8,128)S(1)}, u32[]{:S(2)}, u32[]{:S(2)}) collective-permute-start(f32[4,32,128]{2,1,0:T(8,128)S(1)} %get-tuple-element.84.refs_10_), channel_id=1, source_target_pairs={{0,1},{1,0},{2,3},{3,2},{4,5},{5,4},{6,7},{7,6},{8,9},{9,8},{10,11... | collective-permute-start | bytes 196616 | tf_op jit(solution)/shard_map/ppermute | solution.py:99
  5.6 5.2 %collective-permute-start.1 = (f32[3,8,128]{2,1,0:T(8,128)S(1)}, f32[3,8,128]{2,1,0:T(8,128)S(1)}, u32[]{:S(2)}, u32[]{:S(2)}) collective-permute-start(f32[3,8,128]{2,1,0:T(8,128)S(1)} %get-tuple-element.82.refs_5_), channel_id=1, source_target_pairs={{0,4},{4,0},{8,12},{12,8},{1,5},{5,1},{9,13},{13,9},{2,6},{6,2},{1... | collective-permute-start | bytes 36872 | tf_op jit(solution)/shard_map/ppermute | solution.py:88
  7.3 5.5 %collective-permute-start.2 = (f32[3,8,128]{2,1,0:T(8,128)S(1)}, f32[3,8,128]{2,1,0:T(8,128)S(1)}, u32[]{:S(2)}, u32[]{:S(2)}) collective-permute-start(f32[3,8,128]{2,1,0:T(8,128)S(1)} %get-tuple-element.83.refs_6_), channel_id=1, source_target_pairs={{0,12},{4,8},{8,4},{12,0},{1,13},{5,9},{9,5},{13,1},{2,14},{6,10},... | collective-permute-start | bytes 36872 | tf_op jit(solution)/shard_map/ppermute | solution.py:87
  13.2 4.9 %collective-permute-start.5 = (f32[4,32,128]{2,1,0:T(8,128)S(1)}, f32[4,32,128]{2,1,0:T(8,128)S(1)}, u32[]{:S(2)}, u32[]{:S(2)}) collective-permute-start(f32[4,32,128]{2,1,0:T(8,128)S(1)} %get-tuple-element.90), channel_id=1, source_target_pairs={{0,2},{1,3},{2,0},{3,1},{4,6},{5,7},{6,4},{7,5},{8,10},{9,11},{10,... | collective-permute-start | bytes 196616 | tf_op jit(solution)/shard_map/ppermute | solution.py:99
  14.8 3.3 %collective-permute-start.4 = (f32[4,32,128]{2,1,0:T(8,128)S(1)}, f32[4,32,128]{2,1,0:T(8,128)S(1)}, u32[]{:S(2)}, u32[]{:S(2)}) collective-permute-start(f32[4,32,128]{2,1,0:T(8,128)S(1)} %get-tuple-element.89.refs_4_), channel_id=1, source_target_pairs={{0,1},{1,0},{2,3},{3,2},{4,5},{5,4},{6,7},{7,6},{8,9},{9,8},{10,11... | collective-permute-start | bytes 196616 | tf_op jit(solution)/shard_map/ppermute | solution.py:99
  14.8 3.3 %collective-permute-start.6 = (f32[2,32,128]{2,1,0:T(8,128)S(1)}, f32[2,32,128]{2,1,0:T(8,128)S(1)}, u32[]{:S(2)}, u32[]{:S(2)}) collective-permute-start(f32[2,32,128]{2,1,0:T(8,128)S(1)} %get-tuple-element.91), channel_id=1, source_target_pairs={{0,3},{1,2},{2,1},{3,0},{4,7},{5,6},{6,5},{7,4},{8,11},{9,10},{10,... | collective-permute-start | bytes 98312 | tf_op jit(solution)/shard_map/ppermute | solution.py:99
  18.6 6.1 %collective-permute-start.7 = (f32[4,32,128]{2,1,0:T(8,128)S(1)}, f32[4,32,128]{2,1,0:T(8,128)S(1)}, u32[]{:S(2)}, u32[]{:S(2)}) collective-permute-start(f32[4,32,128]{2,1,0:T(8,128)S(1)} %get-tuple-element.100.refs_4_), channel_id=1, source_target_pairs={{0,16},{16,0},{1,17},{17,1},{2,18},{18,2},{3,19},{19,3},{4,20},{20... | collective-permute-start | bytes 196616 | tf_op jit(solution)/shard_map/ppermute | solution.py:91
  19.2 3.7 %collective-permute-start.8 = (f32[2,8,128]{2,1,0:T(8,128)S(1)}, f32[2,8,128]{2,1,0:T(8,128)S(1)}, u32[]{:S(2)}, u32[]{:S(2)}) collective-permute-start(f32[2,8,128]{2,1,0:T(8,128)S(1)} %get-tuple-element.101.refs_5_), channel_id=1, source_target_pairs={{0,4},{4,0},{8,12},{12,8},{1,5},{5,1},{9,13},{13,9},{2,6},{6,2},{1... | collective-permute-start | bytes 24584 | tf_op jit(solution)/shard_map/ppermute | solution.py:88
  19.2 5.4 %collective-permute-start.9 = (f32[2,8,128]{2,1,0:T(8,128)S(1)}, f32[2,8,128]{2,1,0:T(8,128)S(1)}, u32[]{:S(2)}, u32[]{:S(2)}) collective-permute-start(f32[2,8,128]{2,1,0:T(8,128)S(1)} %get-tuple-element.102.refs_6_), channel_id=1, source_target_pairs={{0,12},{4,8},{8,4},{12,0},{1,13},{5,9},{9,5},{13,1},{2,14},{6,10},... | collective-permute-start | bytes 24584 | tf_op jit(solution)/shard_map/ppermute | solution.py:87
  25.2 4.7 %collective-permute-start.10 = (f32[4,32,128]{2,1,0:T(8,128)S(1)}, f32[4,32,128]{2,1,0:T(8,128)S(1)}, u32[]{:S(2)}, u32[]{:S(2)}) collective-permute-start(f32[4,32,128]{2,1,0:T(8,128)S(1)} %get-tuple-element.108.refs_4_), channel_id=1, source_target_pairs={{0,1},{1,0},{2,3},{3,2},{4,5},{5,4},{6,7},{7,6},{8,9},{9,8},{10,11... | collective-permute-start | bytes 196616 | tf_op jit(solution)/shard_map/ppermute | solution.py:99
  25.2 4.0 %collective-permute-start.11 = (f32[2,32,128]{2,1,0:T(8,128)S(1)}, f32[2,32,128]{2,1,0:T(8,128)S(1)}, u32[]{:S(2)}, u32[]{:S(2)}) collective-permute-start(f32[2,32,128]{2,1,0:T(8,128)S(1)} %get-tuple-element.109), channel_id=1, source_target_pairs={{0,2},{1,3},{2,0},{3,1},{4,6},{5,7},{6,4},{7,5},{8,10},{9,11},{10,... | collective-permute-start | bytes 98312 | tf_op jit(solution)/shard_map/ppermute | solution.py:99
  26.5 3.4 %collective-permute-start.12 = (f32[2,32,128]{2,1,0:T(8,128)S(1)}, f32[2,32,128]{2,1,0:T(8,128)S(1)}, u32[]{:S(2)}, u32[]{:S(2)}) collective-permute-start(f32[2,32,128]{2,1,0:T(8,128)S(1)} %get-tuple-element.110), channel_id=1, source_target_pairs={{0,3},{1,2},{2,1},{3,0},{4,7},{5,6},{6,5},{7,4},{8,11},{9,10},{10,... | collective-permute-start | bytes 98312 | tf_op jit(solution)/shard_map/ppermute | solution.py:99
  30.3 7.2 %collective-permute-start.13 = (f32[4,32,128]{2,1,0:T(8,128)S(1)}, f32[4,32,128]{2,1,0:T(8,128)S(1)}, u32[]{:S(2)}, u32[]{:S(2)}) collective-permute-start(f32[4,32,128]{2,1,0:T(8,128)S(1)} %get-tuple-element.118.refs_4_), channel_id=1, source_target_pairs={{0,16},{16,0},{1,17},{17,1},{2,18},{18,2},{3,19},{19,3},{4,20},{20... | collective-permute-start | bytes 196616 | tf_op jit(solution)/shard_map/ppermute | solution.py:91
  31.9 3.7 %collective-permute-start.14 = (f32[2,8,128]{2,1,0:T(8,128)S(1)}, f32[2,8,128]{2,1,0:T(8,128)S(1)}, u32[]{:S(2)}, u32[]{:S(2)}) collective-permute-start(f32[2,8,128]{2,1,0:T(8,128)S(1)} %get-tuple-element.119.refs_5_), channel_id=1, source_target_pairs={{0,4},{4,0},{8,12},{12,8},{1,5},{5,1},{9,13},{13,9},{2,6},{6,2},{1... | collective-permute-start | bytes 24584 | tf_op jit(solution)/shard_map/ppermute | solution.py:88
  32.1 5.4 %collective-permute-start.15 = (f32[2,8,128]{2,1,0:T(8,128)S(1)}, f32[2,8,128]{2,1,0:T(8,128)S(1)}, u32[]{:S(2)}, u32[]{:S(2)}) collective-permute-start(f32[2,8,128]{2,1,0:T(8,128)S(1)} %get-tuple-element.120.refs_6_), channel_id=1, source_target_pairs={{0,12},{4,8},{8,4},{12,0},{1,13},{5,9},{9,5},{13,1},{2,14},{6,10},... | collective-permute-start | bytes 24584 | tf_op jit(solution)/shard_map/ppermute | solution.py:87
  38.0 4.5 %collective-permute-start.16 = (f32[4,32,128]{2,1,0:T(8,128)S(1)}, f32[4,32,128]{2,1,0:T(8,128)S(1)}, u32[]{:S(2)}, u32[]{:S(2)}) collective-permute-start(f32[4,32,128]{2,1,0:T(8,128)S(1)} %get-tuple-element.129.refs_4_), channel_id=1, source_target_pairs={{0,1},{1,0},{2,3},{3,2},{4,5},{5,4},{6,7},{7,6},{8,9},{9,8},{10,11... | collective-permute-start | bytes 196616 | tf_op jit(solution)/shard_map/ppermute | solution.py:99
  38.1 4.0 %collective-permute-start.17 = (f32[2,32,128]{2,1,0:T(8,128)S(1)}, f32[2,32,128]{2,1,0:T(8,128)S(1)}, u32[]{:S(2)}, u32[]{:S(2)}) collective-permute-start(f32[2,32,128]{2,1,0:T(8,128)S(1)} %get-tuple-element.130), channel_id=1, source_target_pairs={{0,2},{1,3},{2,0},{3,1},{4,6},{5,7},{6,4},{7,5},{8,10},{9,11},{10,... | collective-permute-start | bytes 98312 | tf_op jit(solution)/shard_map/ppermute | solution.py:99
  39.2 3.4 %collective-permute-start.18 = (f32[2,32,128]{2,1,0:T(8,128)S(1)}, f32[2,32,128]{2,1,0:T(8,128)S(1)}, u32[]{:S(2)}, u32[]{:S(2)}) collective-permute-start(f32[2,32,128]{2,1,0:T(8,128)S(1)} %get-tuple-element.131), channel_id=1, source_target_pairs={{0,3},{1,2},{2,1},{3,0},{4,7},{5,6},{6,5},{7,4},{8,11},{9,10},{10,... | collective-permute-start | bytes 98312 | tf_op jit(solution)/shard_map/ppermute | solution.py:99
where the time goes:
time: 43.9 us; the launch traced here: 43.7 us
  starting transfers between devices  20.6 us (47%)
  waiting for transfers between devices  13.4 us (31%)
  Pallas kernels  8.93 us (20%)
  between operations  0.74 us (2%)
    pallas_call x12, Pallas kernels, call(): pl.pallas_call(kernel, out_shape=[jax.ShapeDtypeStruct(s, types[n] if n <...  8.93 us
    ppermute x3, starting transfers between devices, exchange(): got = lax.ppermute(messages[1], self.axis, second)  7.42 us
    ppermute x10, waiting for transfers between devices, to_lev(): return lax.ppermute(message, 'lev', [(i, i ^ m) for i in range(n)])  6.91 us
    ppermute x10, starting transfers between devices, to_lev(): return lax.ppermute(message, 'lev', [(i, i ^ m) for i in range(n)])  6.11 us
    ppermute x3, waiting for transfers between devices, exchange(): got = lax.ppermute(messages[1], self.axis, second)  5.74 us
    ppermute x3, starting transfers between devices, exchange(): return [lax.ppermute(messages[0], self.axis, up)]  5.19 us
    ppermute x3, starting transfers between devices, exchange(): return [lax.ppermute(messages[0], self.axis, first), got]  1.87 us
  transfers between devices with their start and end apart: 19, of which 10 were waited for; matrix products, arithmetic and copies ran while one was open for 0% of the time, Pallas kernels for 9%

commit v1 on v0

--- a/solution.py
+++ b/solution.py
@@ -104,27 +104,29 @@
     return group ^ m if n & (n - 1) == 0 else (group - m) % n
 
 
-def pack_columns(ref, picks, outs):
-    depth, ni, nj = ref.shape
+def pack_columns(ref, picks, outs, b):
+    ni, nj = ref.shape[1:]
     per = nj // ni
-    for b in range(depth // per):
-        turned = ref[b * per : (b + 1) * per].reshape(per * ni, nj).T
-        for c, out in zip(picks, outs):
-            out[b : b + 1, :] = turned[c : c + 1, :]
-
-
-def pack_pressure(press, both_x, both_y):
+    turned = ref[b * per : (b + 1) * per].reshape(per * ni, nj).T
+    for c, out in zip(picks, outs):
+        out[b : b + 1, :] = turned[c : c + 1, :]
+
+
+def pack_pressure(press, both_x, both_y, b):
     ni, nj = press.shape[1:]
+    per = nj // ni
+    here = slice(b * per, (b + 1) * per)
     for r in range(2):
-        both_x[0, r] = press[:, ni - 2 + r, :]
-        both_x[1, r] = press[:, r, :]
-    pack_columns(press, (nj - 2, nj - 1, 0, 1), (both_y.at[0, 0], both_y.at[0, 1], both_y.at[1, 0], both_y.at[1, 1]))
+        both_x[0, r, here] = press[here, ni - 2 + r, :]
+        both_x[1, r, here] = press[here, r, :]
+    outs = (both_y.at[0, 0], both_y.at[0, 1], both_y.at[1, 0], both_y.at[1, 1])
+    pack_columns(press, (nj - 2, nj - 1, 0, 1), outs, b)
 
 
 def first_kernel(hx, hy, *refs):
     refs = list(refs)
     take = lambda n: [refs.pop(0) for _ in range(n)]
-    sources, targets = take(6), take(6)
+    sources, targets = take(3), take(3)
     mx, my = take(hx.count), take(hy.count)
     both_x, both_y, sems = refs
     p, v, u = targets[:3]
@@ -132,10 +134,13 @@
     for copy in copies:
         copy.start()
     ni, nj = p.shape[1:]
+    blocks = range(p.shape[0] // (nj // ni))
     copies[0].wait()
-    pack_pressure(p, both_x, both_y)
+    for b in blocks:
+        pack_pressure(p, both_x, both_y, b)
     copies[1].wait()
-    pack_columns(v, (nj - 1, 0), (both_y.at[0, 2], both_y.at[1, 2]))
+    for b in blocks:
+        pack_columns(v, (nj - 1, 0), (both_y.at[0, 2], both_y.at[1, 2]), b)
     copies[2].wait()
     both_x[0, 2] = u[:, ni - 1, :]
     both_x[1, 2] = u[:, 0, :]
@@ -253,6 +258,17 @@
     return jnp.dot(jnp.concatenate([high, low], 1), matrix, preferred_element_type=F32)
 
 
+def at_lanes(low, high, nj):
+    tile = 8
+    place = lax.broadcasted_iota(jnp.int32, (tile, nj), 0)
+    top = bottom = jnp.zeros((tile, nj), F32)
+    for n, row in enumerate(low):
+        top = jnp.where(place == n, row, top)
+    for n, row in enumerate(high):
+        bottom = jnp.where(place == tile - len(high) + n, row, bottom)
+    return jnp.concatenate([top, jnp.zeros((nj - 2 * tile, nj), F32), bottom], 0).T
+
+
 def add_rows(ref, rows):
     for r, plane in rows:
         ref[:, r, :] = ref[:, r, :] + plane
@@ -262,15 +278,9 @@
     refs = list(refs)
     take = lambda n: [refs.pop(0) for _ in range(n)]
     zonal, merid, press = take(3)
-    if first:
-        vert = take(1)[0]
-    else:
-        uc, vc = take(2)
+    uc, vc = (None, None) if first else take(2)
     zonal_out, merid_out, part = take(3)
-    if first:
-        copy = pltpu.make_async_copy(vert, take(1)[0], refs.pop())
-        copy.start()
-    pe, ue, square = take(3)
+    pe, ue = take(2)
     depth, ni, nj = press.shape
     per = nj // ni
     rows = per * ni
@@ -280,8 +290,6 @@
         ref[:, PAD - 1, :] = edge
         ref[:, PAD + ni, :] = edge
     above, below = slice(PAD + 1, PAD + 1 + ni), slice(PAD - 1, PAD - 1 + ni)
-    if not first:
-        square[...] = jnp.zeros(square.shape, F32)
     for b in range(depth // per):
         here = slice(b * per, (b + 1) * per)
         pe[here, PAD : PAD + ni, :] = press[here]
@@ -294,26 +302,20 @@
         ue[here, PAD : PAD + ni, :] = zonal_out[here]
         v = merid[here].reshape(rows, nj)
         if not first:
-            square[0:1, :] = vc[0, b : b + 1, :]
-            square[nj - 1 : nj, :] = vc[1, b : b + 1, :]
-            v = v + square[...].T
+            v = v + at_lanes((vc[0, b : b + 1, :],), (vc[1, b : b + 1, :],), nj)
         v = v - H_STEP * lane_difference(p, matrix)
         merid_out[here] = v.reshape(per, ni, nj)
         spread = (ue[here, above, :] - ue[here, below, :]).reshape(rows, nj) + lane_difference(v, matrix)
         part[here] = (p - D_STEP * spread).reshape(per, ni, nj)
-    if first:
-        copy.wait()
-
-
-def emit_kernel(zonal, merid, uc, vc, zonal_out, merid_out, square):
+
+
+def emit_kernel(zonal, merid, uc, vc, zonal_out, merid_out):
     depth, ni, nj = zonal.shape
     per = nj // ni
-    square[...] = jnp.zeros(square.shape, F32)
     for b in range(depth // per):
         here = slice(b * per, (b + 1) * per)
-        square[0:1, :] = vc[0, b : b + 1, :]
-        square[nj - 1 : nj, :] = vc[1, b : b + 1, :]
-        merid_out[here] = merid[here] + square[...].T.reshape(per, ni, nj)
+        turned = at_lanes((vc[0, b : b + 1, :],), (vc[1, b : b + 1, :],), nj)
+        merid_out[here] = merid[here] + turned.reshape(per, ni, nj)
         zonal_out[here] = zonal[here]
     add_rows(zonal_out, ((0, uc[0]), (ni - 1, uc[1])))
 
@@ -334,7 +336,7 @@
     if paired and first:
         cf = take(1)[0]
     uh_out, vh_out = (None, None) if final else take(2)
-    square = take(1)[0]
+    rows = take(1)[0]
     depth, ni, nj = part0.shape
     last, half, per = depth - 1, depth // 2, nj // ni
     group = lax.axis_index("lev")
@@ -357,17 +359,17 @@
         vh_out[0], vh_out[1] = v_lo, v_hi
     v_first, v_last = H_STEP * hy.low(ry, 1, even_y), -H_STEP * hy.high(ry, 0, even_y)
     vc[0], vc[1] = v_first, v_last
-    square[...] = jnp.zeros(square.shape, F32)
-    for b in range(depth // per):
-        here = slice(b * per, (b + 1) * per)
-        one = slice(b, b + 1)
-        square[0:1, :] = D_STEP * v_lo[one]
-        square[1:2, :] = D_STEP * v_first[one]
-        square[nj - 2 : nj - 1, :] = -D_STEP * v_last[one]
-        square[nj - 1 : nj, :] = -D_STEP * v_hi[one]
-        part[here] = part0[here] + square[...].T.reshape(per, ni, nj)
     edges = ((0, D_STEP * u_lo), (1, D_STEP * u_first), (ni - 2, -D_STEP * u_last), (ni - 1, -D_STEP * u_hi))
-    add_rows(part, edges)
+    for n, (_, plane) in enumerate(edges):
+        rows[n] = plane
+    blocks = depth // per
+    for b in [x for pair in zip(range(blocks // 2), range(blocks - 1, -1, -1)) for x in pair] + [blocks // 2] * (blocks % 2):
+        here, one = slice(b * per, (b + 1) * per), slice(b, b + 1)
+        low = (D_STEP * v_lo[one], D_STEP * v_first[one])
+        high = (-D_STEP * v_last[one], -D_STEP * v_hi[one])
+        part[here] = part0[here] + at_lanes(low, high, nj).reshape(per, ni, nj)
+        for n, (r, _) in enumerate(edges):
+            part[here, r, :] = part[here, r, :] + rows[n, here]
 
     lo = vert[0] - V_STEP * part[1]
     hi = vert[last] + V_STEP * part[last - 1]
@@ -488,7 +490,7 @@
     if first:
         early, system = system, take(1)[0]
     lv = take(1)[0]
-    depth, _, _ = y.shape
+    depth, ni, nj = y.shape
     group = lax.axis_index("lev")
     if paired:
         if first:
@@ -524,9 +526,12 @@
         for copy in copies:
             copy.wait()
         return
-    lax.fori_loop(0, depth, level, under, unroll=4)
     both_x, both_y = take(2)
-    pack_pressure(press_out, both_x, both_y)
+    w, per = under, nj // ni
+    for k in range(depth):
+        w = level(k, w)
+        if (k + 1) % per == 0:
+            pack_pressure(press_out, both_x, both_y, k // per)
     hx.write(mx, both_x, lax.axis_index("gx") % 2 == 0)
     hy.write(my, both_y, lax.axis_index("gy") % 2 == 0)
 
@@ -538,19 +543,18 @@
     hx = Halo("gx", (depth, nj))
     hy = Halo("gy", (depth // (nj // ni), nj))
     wide = pltpu.VMEM((depth, ni + 2 * PAD, nj), F32)
-    square = pltpu.VMEM((nj, nj), F32)
-
-    inputs = (pressure, meridional, zonal, coupling, surface, lid_flag)
+
+    inputs = (pressure, meridional, zonal)
     results = call(
         functools.partial(first_kernel, hx, hy),
-        [full] * 4 + [surface.shape] * 2 + hx.shapes(3) + hy.shapes(3),
+        [full] * 3 + hx.shapes(3) + hy.shapes(3),
         [pltpu.with_memory_space_constraint(a, pltpu.HBM) for a in inputs],
-        scratch=[hx.scratch(3), hy.scratch(3), pltpu.SemaphoreType.DMA((6,))],
-        spaces=[HBM] * 6,
+        scratch=[hx.scratch(3), hy.scratch(3), pltpu.SemaphoreType.DMA((3,))],
+        spaces=[HBM] * 3,
         types=[a.dtype for a in inputs],
     )
-    pressure, meridional, zonal, coupling, surface, lid_flag = results[:6]
-    ox, oy = results[6 : 6 + hx.count], results[6 + hx.count :]
+    pressure, meridional, zonal = results[:3]
+    ox, oy = results[3 : 3 + hx.count], results[3 + hx.count :]
     ry, rx = hy.exchange(oy), hx.exchange(ox)
     inv, mul, g0, gl, own_s = call(
         functools.partial(factor_kernel, groups), [full] * 4 + [four], [coupling, surface, lid_flag]
@@ -562,17 +566,10 @@
     for substep in range(SUBSTEPS):
         first, final = substep == 0, substep == SUBSTEPS - 1
         args = [zonal, meridional, pressure]
-        args += [pltpu.with_memory_space_constraint(vertical, pltpu.HBM)] if first else [uc, vc]
-        results = call(
-            functools.partial(interior_kernel, first),
-            [full] * (4 if first else 3),
-            args,
-            scratch=[wide, wide, square] + ([pltpu.SemaphoreType.DMA(())] if first else []),
-            spaces=[VMEM] * 3 + [HBM] if first else None,
+        args += [] if first else [uc, vc]
+        zonal, meridional, part = call(
+            functools.partial(interior_kernel, first), [full] * 3, args, scratch=[wide, wide]
         )
-        zonal, meridional, part = results[:3]
-        if first:
-            vertical = results[3]
         args = [part, vertical, inv, mul] + ox + oy + rx + ry
         args += [] if first else [uh, vh]
         if paired:
@@ -582,7 +579,7 @@
         if paired:
             outs += [four if first else two, two] + ([setup] if first else [])
         outs += [] if final else ends
-        results = call(functools.partial(solve_kernel, first, final, hx, hy, groups), outs, args, scratch=[square])
+        results = call(functools.partial(solve_kernel, first, final, hx, hy, groups), outs, args, scratch=[pltpu.VMEM((4,) + hx.plane, F32)])
         y, part, own, uc, vc = results[:5]
         if not final:
             uh, vh = results[-2:]
@@ -593,7 +590,7 @@
         else:
             got = [to_lev(own, m) for m in range(1, groups)]
         if final:
-            zonal, meridional = call(emit_kernel, [full] * 2, [zonal, meridional, uc, vc], scratch=[square])
+            zonal, meridional = call(emit_kernel, [full] * 2, [zonal, meridional, uc, vc])
         args = [y, part, g0, gl, own] + got + [own_s if system is None else system]
         if first and not paired:
             args += [own_s] + got_s

time: 43.9 us -> 43.6 us (level)
  Pallas kernels: 8.93 us -> 8.13 us
  waiting for transfers between devices: 13.4 us -> 13.9 us
    pallas_call x12, Pallas kernels: 8.93 us -> 8.13 us  [call(): pl.pallas_call(kernel, out_shape=[jax.ShapeDtypeStruct(s, types[n] if n <...]
    ppermute x3, waiting for transfers between devices: 5.74 us -> 6.22 us  [exchange(): got = lax.ppermute(messages[1], self.axis, second)]
  transfers between devices with their start and end apart: 19 -> 19, of which waited for: 10 -> 10; matrix products, arithmetic and copies ran while one was open for 0% -> 0% of each run, Pallas kernels for 9% -> 8%
where the time goes in v1:
time: 43.6 us; the launch traced here: 43.4 us
  starting transfers between devices  20.6 us (47%)
  waiting for transfers between devices  13.9 us (32%)
  Pallas kernels  8.13 us (19%)
  between operations  0.76 us (2%)
    pallas_call x12, Pallas kernels, call(): pl.pallas_call(kernel, out_shape=[jax.ShapeDtypeStruct(s, types[n] if n <...  8.13 us
    ppermute x3, starting transfers between devices, exchange(): got = lax.ppermute(messages[1], self.axis, second)  7.42 us
    ppermute x10, waiting for transfers between devices, to_lev(): return lax.ppermute(message, 'lev', [(i, i ^ m) for i in range(n)])  6.92 us
    ppermute x3, waiting for transfers between devices, exchange(): got = lax.ppermute(messages[1], self.axis, second)  6.22 us
    ppermute x10, starting transfers between devices, to_lev(): return lax.ppermute(message, 'lev', [(i, i ^ m) for i in range(n)])  6.11 us
    ppermute x3, starting transfers between devices, exchange(): return [lax.ppermute(messages[0], self.axis, up)]  5.19 us
    ppermute x3, starting transfers between devices, exchange(): return [lax.ppermute(messages[0], self.axis, first), got]  1.87 us
  transfers between devices with their start and end apart: 19, of which 10 were waited for; matrix products, arithmetic and copies ran while one was open for 0% of the time, Pallas kernels for 8%

profile of v1, /device:TPU:0, one launch (start us, length us, event | category | flops | bytes accessed | tf_op | source)
XLA Modules:
  0.0 43.4 jit_solution(7811131557851178702)
XLA Ops:
  0.7 1.6 %shard_map.102 = (f32[32,32,128]{2,1,0:T(8,128)S(1)}, f32[32,32,128]{2,1,0:T(8,128)S(1)}, f32[32,32,128]{2,1,0:T(8,128)S(1)}, f32[6,32,128]{2,1,0:T(8,128)S(1)},...) custom-call(f32[32,32,128]{2,1,0:T(8,128)} %refs_0_.1, f32[32,32,128]{2,1,0:T(8,128)} %refs_1_.2, f32[32,32,128]{2,1,0:T(8,128)} %refs_2_.1), custom_call_target="tpu_custom_call" | custom-call | tf_op jit(solution)/shard_map/pallas_call | solution.py:24
  2.2 3.0 %collective-permute-start = (f32[6,32,128]{2,1,0:T(8,128)S(1)}, f32[6,32,128]{2,1,0:T(8,128)S(1)}, u32[]{:S(2)}, u32[]{:S(2)}) collective-permute-start(f32[6,32,128]{2,1,0:T(8,128)S(1)} %get-tuple-element.73.refs_4_), channel_id=1, source_target_pairs={{0,16},{16,0},{1,17},{17,1},{2,18},{18,2},{3,19},{19,3},{4,20},{20... | collective-permute-start | bytes 294920 | tf_op jit(solution)/shard_map/ppermute | solution.py:91
  5.3 0.3 shard_map.104
  5.6 0.1 collective-permute-start.3
  5.6 1.6 %collective-permute-start.1 = (f32[3,8,128]{2,1,0:T(8,128)S(1)}, f32[3,8,128]{2,1,0:T(8,128)S(1)}, u32[]{:S(2)}, u32[]{:S(2)}) collective-permute-start(f32[3,8,128]{2,1,0:T(8,128)S(1)} %get-tuple-element.74.refs_5_), channel_id=1, source_target_pairs={{0,4},{4,0},{8,12},{12,8},{1,5},{5,1},{9,13},{13,9},{2,6},{6,2},{1... | collective-permute-start | bytes 36872 | tf_op jit(solution)/shard_map/ppermute | solution.py:88
  7.3 2.5 %collective-permute-start.2 = (f32[3,8,128]{2,1,0:T(8,128)S(1)}, f32[3,8,128]{2,1,0:T(8,128)S(1)}, u32[]{:S(2)}, u32[]{:S(2)}) collective-permute-start(f32[3,8,128]{2,1,0:T(8,128)S(1)} %get-tuple-element.75.refs_6_), channel_id=1, source_target_pairs={{0,12},{4,8},{8,4},{12,0},{1,13},{5,9},{9,5},{13,1},{2,14},{6,10},... | collective-permute-start | bytes 36872 | tf_op jit(solution)/shard_map/ppermute | solution.py:87
  9.8 0.6 %shard_map.103 = (f32[32,32,128]{2,1,0:T(8,128)S(1)}, f32[32,32,128]{2,1,0:T(8,128)S(1)}, f32[32,32,128]{2,1,0:T(8,128)S(1)}) custom-call(f32[32,32,128]{2,1,0:T(8,128)S(1)} %get-tuple-element.65.refs_0_, f32[32,32,128]{2,1,0:T(8,128)S(1)} %get-tuple-element.66.refs_1_, f32[32,32,128]{2,1,0:T(8,128)S(1)} %get-tuple-element.67.refs_2_), custom_call_target="tpu_custom_call" | custom-call | tf_op jit(solution)/shard_map/pallas_call | solution.py:24
  10.4 0.0 collective-permute-done.1.refs_8_
  10.4 2.4 %collective-permute-done.2.refs_9_ = f32[3,8,128]{2,1,0:T(8,128)S(1)} collective-permute-done((f32[3,8,128]{2,1,0:T(8,128)S(1)}, f32[3,8,128]{2,1,0:T(8,128)S(1)}, u32[]{:S(2)}, u32[]{:S(2)}) %collective-permute-start.2) | collective-permute-done | bytes 12320 | tf_op jit(solution)/shard_map/ppermute | solution.py:87
  12.8 0.0 collective-permute-done.3.refs_11_
  12.8 0.0 collective-permute-done.refs_7_
  12.8 0.5 %shard_map.105 = (f32[32,32,128]{2,1,0:T(8,128)S(1)}, f32[32,32,128]{2,1,0:T(8,128)S(1)}, f32[4,32,128]{2,1,0:T(8,128)S(1)}, f32[2,32,128]{2,1,0:T(8,128)S(1)}, ...) custom-call(f32[32,32,128]{2,1,0:T(8,128)S(1)} %get-tuple-element.70, ...), custom_call_target="tpu_custom_call" | custom-call | tf_op jit(solution)/shard_map/pallas_call | solution.py:24
  13.3 1.6 %collective-permute-start.5 = (f32[4,32,128]{2,1,0:T(8,128)S(1)}, f32[4,32,128]{2,1,0:T(8,128)S(1)}, u32[]{:S(2)}, u32[]{:S(2)}) collective-permute-start(f32[4,32,128]{2,1,0:T(8,128)S(1)} %get-tuple-element.82), channel_id=1, source_target_pairs={{0,2},{1,3},{2,0},{3,1},{4,6},{5,7},{6,4},{7,5},{8,10},{9,11},{10,... | collective-permute-start | bytes 196616 | tf_op jit(solution)/shard_map/ppermute | solution.py:99
  14.8 0.0 collective-permute-start.4
  14.8 0.6 %collective-permute-start.6 = (f32[2,32,128]{2,1,0:T(8,128)S(1)}, f32[2,32,128]{2,1,0:T(8,128)S(1)}, u32[]{:S(2)}, u32[]{:S(2)}) collective-permute-start(f32[2,32,128]{2,1,0:T(8,128)S(1)} %get-tuple-element.83), channel_id=1, source_target_pairs={{0,3},{1,2},{2,1},{3,0},{4,7},{5,6},{6,5},{7,4},{8,11},{9,10},{10,... | collective-permute-start | bytes 98312 | tf_op jit(solution)/shard_map/ppermute | solution.py:99
  15.5 2.7 %collective-permute-done.6.refs_7_ = f32[2,32,128]{2,1,0:T(8,128)S(1)} collective-permute-done((f32[2,32,128]{2,1,0:T(8,128)S(1)}, f32[2,32,128]{2,1,0:T(8,128)S(1)}, u32[]{:S(2)}, u32[]{:S(2)}) %collective-permute-start.6) | collective-permute-done | bytes 32800 | tf_op jit(solution)/shard_map/ppermute | solution.py:99
  18.2 0.0 collective-permute-done.5.refs_6_
  18.2 0.0 collective-permute-done.4.refs_5_
  18.2 0.3 shard_map.106
  18.5 0.6 %collective-permute-start.7 = (f32[4,32,128]{2,1,0:T(8,128)S(1)}, f32[4,32,128]{2,1,0:T(8,128)S(1)}, u32[]{:S(2)}, u32[]{:S(2)}) collective-permute-start(f32[4,32,128]{2,1,0:T(8,128)S(1)} %get-tuple-element.92.refs_4_), channel_id=1, source_target_pairs={{0,16},{16,0},{1,17},{17,1},{2,18},{18,2},{3,19},{19,3},{4,20},{20... | collective-permute-start | bytes 196616 | tf_op jit(solution)/shard_map/ppermute | solution.py:91
  19.1 2.5 %collective-permute-start.9 = (f32[2,8,128]{2,1,0:T(8,128)S(1)}, f32[2,8,128]{2,1,0:T(8,128)S(1)}, u32[]{:S(2)}, u32[]{:S(2)}) collective-permute-start(f32[2,8,128]{2,1,0:T(8,128)S(1)} %get-tuple-element.94.refs_6_), channel_id=1, source_target_pairs={{0,12},{4,8},{8,4},{12,0},{1,13},{5,9},{9,5},{13,1},{2,14},{6,10},... | collective-permute-start | bytes 24584 | tf_op jit(solution)/shard_map/ppermute | solution.py:87
  21.6 0.7 %shard_map.107 = (f32[32,32,128]{2,1,0:T(8,128)S(1)}, f32[32,32,128]{2,1,0:T(8,128)S(1)}, f32[32,32,128]{2,1,0:T(8,128)S(1)}) custom-call(f32[32,32,128]{2,1,0:T(8,128)S(1)} %get-tuple-element.68.refs_0_, f32[32,32,128]{2,1,0:T(8,128)S(1)} %get-tuple-element.69.refs_1_, f32[32,32,128]{2,1,0:T(8,128)S(1)} %get-tuple-element.85.refs_2_, ...), custom_call_target="tpu_custom_call" | custom-call | tf_op jit(solution)/shard_map/pallas_call | solution.py:24
  22.3 0.5 %collective-permute-done.8.refs_8_ = f32[2,8,128]{2,1,0:T(8,128)S(1)} collective-permute-done((f32[2,8,128]{2,1,0:T(8,128)S(1)}, f32[2,8,128]{2,1,0:T(8,128)S(1)}, u32[]{:S(2)}, u32[]{:S(2)}) %collective-permute-start.8) | collective-permute-done | bytes 8224 | tf_op jit(solution)/shard_map/ppermute | solution.py:88
  22.8 1.8 %collective-permute-done.9.refs_9_ = f32[2,8,128]{2,1,0:T(8,128)S(1)} collective-permute-done((f32[2,8,128]{2,1,0:T(8,128)S(1)}, f32[2,8,128]{2,1,0:T(8,128)S(1)}, u32[]{:S(2)}, u32[]{:S(2)}) %collective-permute-start.9) | collective-permute-done | bytes 8224 | tf_op jit(solution)/shard_map/ppermute | solution.py:87
  24.6 0.0 collective-permute-done.7.refs_7_
  24.6 0.4 %shard_map.108 = (f32[32,32,128]{2,1,0:T(8,128)S(1)}, f32[32,32,128]{2,1,0:T(8,128)S(1)}, f32[4,32,128]{2,1,0:T(8,128)S(1)}, f32[2,32,128]{2,1,0:T(8,128)S(1)}, ...) custom-call(f32[32,32,128]{2,1,0:T(8,128)S(1)} %get-tuple-element.90, ...), custom_call_target="tpu_custom_call" | custom-call | tf_op jit(solution)/shard_map/pallas_call | solution.py:24
  25.0 0.1 collective-permute-start.10
  25.1 1.3 %collective-permute-start.11 = (f32[2,32,128]{2,1,0:T(8,128)S(1)}, f32[2,32,128]{2,1,0:T(8,128)S(1)}, u32[]{:S(2)}, u32[]{:S(2)}) collective-permute-start(f32[2,32,128]{2,1,0:T(8,128)S(1)} %get-tuple-element.101), channel_id=1, source_target_pairs={{0,2},{1,3},{2,0},{3,1},{4,6},{5,7},{6,4},{7,5},{8,10},{9,11},{10,... | collective-permute-start | bytes 98312 | tf_op jit(solution)/shard_map/ppermute | solution.py:99
  26.4 0.6 %collective-permute-start.12 = (f32[2,32,128]{2,1,0:T(8,128)S(1)}, f32[2,32,128]{2,1,0:T(8,128)S(1)}, u32[]{:S(2)}, u32[]{:S(2)}) collective-permute-start(f32[2,32,128]{2,1,0:T(8,128)S(1)} %get-tuple-element.102), channel_id=1, source_target_pairs={{0,3},{1,2},{2,1},{3,0},{4,7},{5,6},{6,5},{7,4},{8,11},{9,10},{10,... | collective-permute-start | bytes 98312 | tf_op jit(solution)/shard_map/ppermute | solution.py:99
  27.0 2.1 %collective-permute-done.11.refs_6_ = f32[2,32,128]{2,1,0:T(8,128)S(1)} collective-permute-done((f32[2,32,128]{2,1,0:T(8,128)S(1)}, f32[2,32,128]{2,1,0:T(8,128)S(1)}, u32[]{:S(2)}, u32[]{:S(2)}) %collective-permute-start.11) | collective-permute-done | bytes 32800 | tf_op jit(solution)/shard_map/ppermute | solution.py:99
  29.1 0.6 %collective-permute-done.12.refs_7_ = f32[2,32,128]{2,1,0:T(8,128)S(1)} collective-permute-done((f32[2,32,128]{2,1,0:T(8,128)S(1)}, f32[2,32,128]{2,1,0:T(8,128)S(1)}, u32[]{:S(2)}, u32[]{:S(2)}) %collective-permute-start.12) | collective-permute-done | bytes 32800 | tf_op jit(solution)/shard_map/ppermute | solution.py:99
  29.7 0.0 collective-permute-done.10.refs_5_
  29.7 0.3 shard_map.109
  30.1 1.6 %collective-permute-start.13 = (f32[4,32,128]{2,1,0:T(8,128)S(1)}, f32[4,32,128]{2,1,0:T(8,128)S(1)}, u32[]{:S(2)}, u32[]{:S(2)}) collective-permute-start(f32[4,32,128]{2,1,0:T(8,128)S(1)} %get-tuple-element.110.refs_4_), channel_id=1, source_target_pairs={{0,16},{16,0},{1,17},{17,1},{2,18},{18,2},{3,19},{19,3},{4,20},{20... | collective-permute-start | bytes 196616 | tf_op jit(solution)/shard_map/ppermute | solution.py:91
  31.6 0.2 collective-permute-start.14
  31.9 2.5 %collective-permute-start.15 = (f32[2,8,128]{2,1,0:T(8,128)S(1)}, f32[2,8,128]{2,1,0:T(8,128)S(1)}, u32[]{:S(2)}, u32[]{:S(2)}) collective-permute-start(f32[2,8,128]{2,1,0:T(8,128)S(1)} %get-tuple-element.112.refs_6_), channel_id=1, source_target_pairs={{0,12},{4,8},{8,4},{12,0},{1,13},{5,9},{9,5},{13,1},{2,14},{6,10},... | collective-permute-start | bytes 24584 | tf_op jit(solution)/shard_map/ppermute | solution.py:87
  34.3 0.7 %shard_map.110 = (f32[32,32,128]{2,1,0:T(8,128)S(1)}, f32[32,32,128]{2,1,0:T(8,128)S(1)}, f32[32,32,128]{2,1,0:T(8,128)S(1)}) custom-call(f32[32,32,128]{2,1,0:T(8,128)S(1)} %get-tuple-element.88.refs_0_, f32[32,32,128]{2,1,0:T(8,128)S(1)} %get-tuple-element.89.refs_1_, f32[32,32,128]{2,1,0:T(8,128)S(1)} %get-tuple-element.103.refs_2_, ...), custom_call_target="tpu_custom_call" | custom-call | tf_op jit(solution)/shard_map/pallas_call | solution.py:24
  35.0 0.3 collective-permute-done.14.refs_8_
  35.3 2.0 %collective-permute-done.15.refs_9_ = f32[2,8,128]{2,1,0:T(8,128)S(1)} collective-permute-done((f32[2,8,128]{2,1,0:T(8,128)S(1)}, f32[2,8,128]{2,1,0:T(8,128)S(1)}, u32[]{:S(2)}, u32[]{:S(2)}) %collective-permute-start.15) | collective-permute-done | bytes 8224 | tf_op jit(solution)/shard_map/ppermute | solution.py:87
  37.3 0.0 collective-permute-done.13.refs_7_
  37.3 0.4 %shard_map.111 = (f32[32,32,128]{2,1,0:T(8,128)S(1)}, f32[32,32,128]{2,1,0:T(8,128)S(1)}, f32[4,32,128]{2,1,0:T(8,128)S(1)}, f32[2,32,128]{2,1,0:T(8,128)S(1)}, ...) custom-call(f32[32,32,128]{2,1,0:T(8,128)S(1)} %get-tuple-element.108.refs_0_, ...), custom_call_target="tpu_custom_call" | custom-call | tf_op jit(solution)/shard_map/pallas_call | solution.py:24
  37.8 0.1 collective-permute-start.16
  37.8 1.1 %collective-permute-start.17 = (f32[2,32,128]{2,1,0:T(8,128)S(1)}, f32[2,32,128]{2,1,0:T(8,128)S(1)}, u32[]{:S(2)}, u32[]{:S(2)}) collective-permute-start(f32[2,32,128]{2,1,0:T(8,128)S(1)} %get-tuple-element.122), channel_id=1, source_target_pairs={{0,2},{1,3},{2,0},{3,1},{4,6},{5,7},{6,4},{7,5},{8,10},{9,11},{10,... | collective-permute-start | bytes 98312 | tf_op jit(solution)/shard_map/ppermute | solution.py:99
  38.9 0.8 %collective-permute-start.18 = (f32[2,32,128]{2,1,0:T(8,128)S(1)}, f32[2,32,128]{2,1,0:T(8,128)S(1)}, u32[]{:S(2)}, u32[]{:S(2)}) collective-permute-start(f32[2,32,128]{2,1,0:T(8,128)S(1)} %get-tuple-element.123), channel_id=1, source_target_pairs={{0,3},{1,2},{2,1},{3,0},{4,7},{5,6},{6,5},{7,4},{8,11},{9,10},{10,... | collective-permute-start | bytes 98312 | tf_op jit(solution)/shard_map/ppermute | solution.py:99
  39.7 1.2 %shard_map.112 = (f32[32,32,128]{2,1,0:T(8,128)}, f32[32,32,128]{2,1,0:T(8,128)}) custom-call(f32[32,32,128]{2,1,0:T(8,128)S(1)} %get-tuple-element.106.zonal, f32[32,32,128]{2,1,0:T(8,128)S(1)} %get-tuple-element.107.merid, f32[2,32,128]{2,1,0:T(8,128)S(1)} %get-tuple-element.115.uc, f32[2,8,128]{2,1,0:T(8,128)S(1)} %get-tuple-element.116.vc), custom_call_target="tpu_custom_call" | custom-call | tf_op jit(solution)/shard_map/pallas_call | solution.py:24
  40.9 0.9 %collective-permute-done.17.refs_6_ = f32[2,32,128]{2,1,0:T(8,128)S(1)} collective-permute-done((f32[2,32,128]{2,1,0:T(8,128)S(1)}, f32[2,32,128]{2,1,0:T(8,128)S(1)}, u32[]{:S(2)}, u32[]{:S(2)}) %collective-permute-start.17) | collective-permute-done | bytes 32800 | tf_op jit(solution)/shard_map/ppermute | solution.py:99
  41.8 0.5 %collective-permute-done.18.refs_7_ = f32[2,32,128]{2,1,0:T(8,128)S(1)} collective-permute-done((f32[2,32,128]{2,1,0:T(8,128)S(1)}, f32[2,32,128]{2,1,0:T(8,128)S(1)}, u32[]{:S(2)}, u32[]{:S(2)}) %collective-permute-start.18) | collective-permute-done | bytes 32800 | tf_op jit(solution)/shard_map/ppermute | solution.py:99
  42.3 1.1 %shard_map.113 = (f32[32,32,128]{2,1,0:T(8,128)}, f32[32,32,128]{2,1,0:T(8,128)}) custom-call(f32[32,32,128]{2,1,0:T(8,128)S(1)} %get-tuple-element.119.refs_0_, f32[32,32,128]{2,1,0:T(8,128)S(1)} %get-tuple-element.120.refs_1_, f32[32,32,128]{2,1,0:T(8,128)S(1)} %get-tuple-element.79.refs_2_, f32[32,32,128]{2,1,0:T(8,128)S(1)} %get-tuple-element.80.refs_3_, ...), custom_call_target="tpu_custom_call" | custom-call | tf_op jit(solution)/shard_map/pallas_call | solution.py:24
  (10 shorter events, 0.0 us)
Async XLA Ops:
  0.6 4.6 %copy-start.3 = (s32[32,128]{1,0:T(8,128)S(1)}, s32[32,128]{1,0:T(8,128)}, u32[]{:S(2)}) copy-start(s32[32,128]{1,0:T(8,128)} %lid.1) | copy-start | bytes 49156
  0.6 4.6 %copy-start.2 = (s32[32,128]{1,0:T(8,128)S(1)}, s32[32,128]{1,0:T(8,128)}, u32[]{:S(2)}) copy-start(s32[32,128]{1,0:T(8,128)} %surface.1) | copy-start | bytes 49156
  0.7 4.6 %copy-start.1 = (f32[32,32,128]{2,1,0:T(8,128)S(1)}, f32[32,32,128]{2,1,0:T(8,128)}, u32[]{:S(2)}) copy-start(f32[32,32,128]{2,1,0:T(8,128)} %c.1) | copy-start | bytes 1572868
  2.2 10.6 %collective-permute-start = (f32[6,32,128]{2,1,0:T(8,128)S(1)}, f32[6,32,128]{2,1,0:T(8,128)S(1)}, u32[]{:S(2)}, u32[]{:S(2)}) collective-permute-start(f32[6,32,128]{2,1,0:T(8,128)S(1)} %get-tuple-element.73.refs_4_), channel_id=1, source_target_pairs={{0,16},{16,0},{1,17},{17,1},{2,18},{18,2},{3,19},{19,3},{4,20},{20... | collective-permute-start | bytes 294920 | tf_op jit(solution)/shard_map/ppermute | solution.py:91
  5.6 7.2 %collective-permute-start.3 = (f32[4,32,128]{2,1,0:T(8,128)S(1)}, f32[4,32,128]{2,1,0:T(8,128)S(1)}, u32[]{:S(2)}, u32[]{:S(2)}) collective-permute-start(f32[4,32,128]{2,1,0:T(8,128)S(1)} %get-tuple-element.76.refs_10_), channel_id=1, source_target_pairs={{0,1},{1,0},{2,3},{3,2},{4,5},{5,4},{6,7},{7,6},{8,9},{9,8},{10,11... | collective-permute-start | bytes 196616 | tf_op jit(solution)/shard_map/ppermute | solution.py:99
  5.6 4.7 %collective-permute-start.1 = (f32[3,8,128]{2,1,0:T(8,128)S(1)}, f32[3,8,128]{2,1,0:T(8,128)S(1)}, u32[]{:S(2)}, u32[]{:S(2)}) collective-permute-start(f32[3,8,128]{2,1,0:T(8,128)S(1)} %get-tuple-element.74.refs_5_), channel_id=1, source_target_pairs={{0,4},{4,0},{8,12},{12,8},{1,5},{5,1},{9,13},{13,9},{2,6},{6,2},{1... | collective-permute-start | bytes 36872 | tf_op jit(solution)/shard_map/ppermute | solution.py:88
  7.3 5.5 %collective-permute-start.2 = (f32[3,8,128]{2,1,0:T(8,128)S(1)}, f32[3,8,128]{2,1,0:T(8,128)S(1)}, u32[]{:S(2)}, u32[]{:S(2)}) collective-permute-start(f32[3,8,128]{2,1,0:T(8,128)S(1)} %get-tuple-element.75.refs_6_), channel_id=1, source_target_pairs={{0,12},{4,8},{8,4},{12,0},{1,13},{5,9},{9,5},{13,1},{2,14},{6,10},... | collective-permute-start | bytes 36872 | tf_op jit(solution)/shard_map/ppermute | solution.py:87
  9.8 3.0 %copy-start = (f32[32,32,128]{2,1,0:T(8,128)S(1)}, f32[32,32,128]{2,1,0:T(8,128)}, u32[]{:S(2)}) copy-start(f32[32,32,128]{2,1,0:T(8,128)} %refs_1_.3) | copy-start | bytes 1572868
  13.3 4.9 %collective-permute-start.5 = (f32[4,32,128]{2,1,0:T(8,128)S(1)}, f32[4,32,128]{2,1,0:T(8,128)S(1)}, u32[]{:S(2)}, u32[]{:S(2)}) collective-permute-start(f32[4,32,128]{2,1,0:T(8,128)S(1)} %get-tuple-element.82), channel_id=1, source_target_pairs={{0,2},{1,3},{2,0},{3,1},{4,6},{5,7},{6,4},{7,5},{8,10},{9,11},{10,... | collective-permute-start | bytes 196616 | tf_op jit(solution)/shard_map/ppermute | solution.py:99
  14.8 3.3 %collective-permute-start.4 = (f32[4,32,128]{2,1,0:T(8,128)S(1)}, f32[4,32,128]{2,1,0:T(8,128)S(1)}, u32[]{:S(2)}, u32[]{:S(2)}) collective-permute-start(f32[4,32,128]{2,1,0:T(8,128)S(1)} %get-tuple-element.81.refs_4_), channel_id=1, source_target_pairs={{0,1},{1,0},{2,3},{3,2},{4,5},{5,4},{6,7},{7,6},{8,9},{9,8},{10,11... | collective-permute-start | bytes 196616 | tf_op jit(solution)/shard_map/ppermute | solution.py:99
  14.8 3.3 %collective-permute-start.6 = (f32[2,32,128]{2,1,0:T(8,128)S(1)}, f32[2,32,128]{2,1,0:T(8,128)S(1)}, u32[]{:S(2)}, u32[]{:S(2)}) collective-permute-start(f32[2,32,128]{2,1,0:T(8,128)S(1)} %get-tuple-element.83), channel_id=1, source_target_pairs={{0,3},{1,2},{2,1},{3,0},{4,7},{5,6},{6,5},{7,4},{8,11},{9,10},{10,... | collective-permute-start | bytes 98312 | tf_op jit(solution)/shard_map/ppermute | solution.py:99
  18.5 6.1 %collective-permute-start.7 = (f32[4,32,128]{2,1,0:T(8,128)S(1)}, f32[4,32,128]{2,1,0:T(8,128)S(1)}, u32[]{:S(2)}, u32[]{:S(2)}) collective-permute-start(f32[4,32,128]{2,1,0:T(8,128)S(1)} %get-tuple-element.92.refs_4_), channel_id=1, source_target_pairs={{0,16},{16,0},{1,17},{17,1},{2,18},{18,2},{3,19},{19,3},{4,20},{20... | collective-permute-start | bytes 196616 | tf_op jit(solution)/shard_map/ppermute | solution.py:91
  19.1 3.7 %collective-permute-start.8 = (f32[2,8,128]{2,1,0:T(8,128)S(1)}, f32[2,8,128]{2,1,0:T(8,128)S(1)}, u32[]{:S(2)}, u32[]{:S(2)}) collective-permute-start(f32[2,8,128]{2,1,0:T(8,128)S(1)} %get-tuple-element.93.refs_5_), channel_id=1, source_target_pairs={{0,4},{4,0},{8,12},{12,8},{1,5},{5,1},{9,13},{13,9},{2,6},{6,2},{1... | collective-permute-start | bytes 24584 | tf_op jit(solution)/shard_map/ppermute | solution.py:88
  19.1 5.4 %collective-permute-start.9 = (f32[2,8,128]{2,1,0:T(8,128)S(1)}, f32[2,8,128]{2,1,0:T(8,128)S(1)}, u32[]{:S(2)}, u32[]{:S(2)}) collective-permute-start(f32[2,8,128]{2,1,0:T(8,128)S(1)} %get-tuple-element.94.refs_6_), channel_id=1, source_target_pairs={{0,12},{4,8},{8,4},{12,0},{1,13},{5,9},{9,5},{13,1},{2,14},{6,10},... | collective-permute-start | bytes 24584 | tf_op jit(solution)/shard_map/ppermute | solution.py:87
  25.0 4.7 %collective-permute-start.10 = (f32[4,32,128]{2,1,0:T(8,128)S(1)}, f32[4,32,128]{2,1,0:T(8,128)S(1)}, u32[]{:S(2)}, u32[]{:S(2)}) collective-permute-start(f32[4,32,128]{2,1,0:T(8,128)S(1)} %get-tuple-element.100.refs_4_), channel_id=1, source_target_pairs={{0,1},{1,0},{2,3},{3,2},{4,5},{5,4},{6,7},{7,6},{8,9},{9,8},{10,11... | collective-permute-start | bytes 196616 | tf_op jit(solution)/shard_map/ppermute | solution.py:99
  25.1 4.0 %collective-permute-start.11 = (f32[2,32,128]{2,1,0:T(8,128)S(1)}, f32[2,32,128]{2,1,0:T(8,128)S(1)}, u32[]{:S(2)}, u32[]{:S(2)}) collective-permute-start(f32[2,32,128]{2,1,0:T(8,128)S(1)} %get-tuple-element.101), channel_id=1, source_target_pairs={{0,2},{1,3},{2,0},{3,1},{4,6},{5,7},{6,4},{7,5},{8,10},{9,11},{10,... | collective-permute-start | bytes 98312 | tf_op jit(solution)/shard_map/ppermute | solution.py:99
  26.4 3.4 %collective-permute-start.12 = (f32[2,32,128]{2,1,0:T(8,128)S(1)}, f32[2,32,128]{2,1,0:T(8,128)S(1)}, u32[]{:S(2)}, u32[]{:S(2)}) collective-permute-start(f32[2,32,128]{2,1,0:T(8,128)S(1)} %get-tuple-element.102), channel_id=1, source_target_pairs={{0,3},{1,2},{2,1},{3,0},{4,7},{5,6},{6,5},{7,4},{8,11},{9,10},{10,... | collective-permute-start | bytes 98312 | tf_op jit(solution)/shard_map/ppermute | solution.py:99
  30.1 7.2 %collective-permute-start.13 = (f32[4,32,128]{2,1,0:T(8,128)S(1)}, f32[4,32,128]{2,1,0:T(8,128)S(1)}, u32[]{:S(2)}, u32[]{:S(2)}) collective-permute-start(f32[4,32,128]{2,1,0:T(8,128)S(1)} %get-tuple-element.110.refs_4_), channel_id=1, source_target_pairs={{0,16},{16,0},{1,17},{17,1},{2,18},{18,2},{3,19},{19,3},{4,20},{20... | collective-permute-start | bytes 196616 | tf_op jit(solution)/shard_map/ppermute | solution.py:91
  31.6 3.7 %collective-permute-start.14 = (f32[2,8,128]{2,1,0:T(8,128)S(1)}, f32[2,8,128]{2,1,0:T(8,128)S(1)}, u32[]{:S(2)}, u32[]{:S(2)}) collective-permute-start(f32[2,8,128]{2,1,0:T(8,128)S(1)} %get-tuple-element.111.refs_5_), channel_id=1, source_target_pairs={{0,4},{4,0},{8,12},{12,8},{1,5},{5,1},{9,13},{13,9},{2,6},{6,2},{1... | collective-permute-start | bytes 24584 | tf_op jit(solution)/shard_map/ppermute | solution.py:88
  31.9 5.4 %collective-permute-start.15 = (f32[2,8,128]{2,1,0:T(8,128)S(1)}, f32[2,8,128]{2,1,0:T(8,128)S(1)}, u32[]{:S(2)}, u32[]{:S(2)}) collective-permute-start(f32[2,8,128]{2,1,0:T(8,128)S(1)} %get-tuple-element.112.refs_6_), channel_id=1, source_target_pairs={{0,12},{4,8},{8,4},{12,0},{1,13},{5,9},{9,5},{13,1},{2,14},{6,10},... | collective-permute-start | bytes 24584 | tf_op jit(solution)/shard_map/ppermute | solution.py:87
  37.8 4.5 %collective-permute-start.16 = (f32[4,32,128]{2,1,0:T(8,128)S(1)}, f32[4,32,128]{2,1,0:T(8,128)S(1)}, u32[]{:S(2)}, u32[]{:S(2)}) collective-permute-start(f32[4,32,128]{2,1,0:T(8,128)S(1)} %get-tuple-element.121.refs_4_), channel_id=1, source_target_pairs={{0,1},{1,0},{2,3},{3,2},{4,5},{5,4},{6,7},{7,6},{8,9},{9,8},{10,11... | collective-permute-start | bytes 196616 | tf_op jit(solution)/shard_map/ppermute | solution.py:99
  37.8 4.0 %collective-permute-start.17 = (f32[2,32,128]{2,1,0:T(8,128)S(1)}, f32[2,32,128]{2,1,0:T(8,128)S(1)}, u32[]{:S(2)}, u32[]{:S(2)}) collective-permute-start(f32[2,32,128]{2,1,0:T(8,128)S(1)} %get-tuple-element.122), channel_id=1, source_target_pairs={{0,2},{1,3},{2,0},{3,1},{4,6},{5,7},{6,4},{7,5},{8,10},{9,11},{10,... | collective-permute-start | bytes 98312 | tf_op jit(solution)/shard_map/ppermute | solution.py:99
  38.9 3.4 %collective-permute-start.18 = (f32[2,32,128]{2,1,0:T(8,128)S(1)}, f32[2,32,128]{2,1,0:T(8,128)S(1)}, u32[]{:S(2)}, u32[]{:S(2)}) collective-permute-start(f32[2,32,128]{2,1,0:T(8,128)S(1)} %get-tuple-element.123), channel_id=1, source_target_pairs={{0,3},{1,2},{2,1},{3,0},{4,7},{5,6},{6,5},{7,4},{8,11},{9,10},{10,... | collective-permute-start | bytes 98312 | tf_op jit(solution)/shard_map/ppermute | solution.py:99

commit v2 on v1

--- a/solution.py
+++ b/solution.py
@@ -37,7 +37,6 @@
         self.axis, self.plane = axis, plane
         self.n = lax.axis_size(axis)
         self.count = 1 if self.n <= 2 else 2
-        self.swap = self.n > 2 and self.n % 2 == 0
 
     def shapes(self, rows):
         return [(2 * rows,) + self.plane] if self.count == 1 else [(rows,) + self.plane] * 2
@@ -45,52 +44,37 @@
     def scratch(self, rows):
         return pltpu.VMEM((2, rows) + self.plane, F32)
 
-    def write(self, refs, both, even):
+    def write(self, refs, both):
         rows = both.shape[1]
         if self.count == 1:
             refs[0][:rows] = both[0]
             refs[0][rows:] = both[1]
-        elif self.swap:
-            refs[0][...] = jnp.where(even, both[0], both[1])
-            refs[1][...] = jnp.where(even, both[1], both[0])
         else:
             refs[0][...] = both[0]
             refs[1][...] = both[1]
 
-    def up(self, refs, r, even):
-        if self.swap:
-            return jnp.where(even, refs[0][r], refs[1][r])
+    def up(self, refs, r):
         return refs[0][r]
 
-    def down(self, refs, r, even):
-        if self.swap:
-            return jnp.where(even, refs[1][r], refs[0][r])
+    def down(self, refs, r):
         return refs[0][refs[0].shape[0] // 2 + r] if self.count == 1 else refs[1][r]
 
-    def low(self, refs, r, even):
-        if self.swap:
-            return jnp.where(even, refs[1][r], refs[0][r])
+    def low(self, refs, r):
         return refs[0][r]
 
-    def high(self, refs, r, even):
-        if self.swap:
-            return jnp.where(even, refs[0][r], refs[1][r])
+    def high(self, refs, r):
         return refs[0][refs[0].shape[0] // 2 + r] if self.count == 1 else refs[1][r]
 
     def exchange(self, messages):
         n = self.n
         if n == 1:
             return messages
-        if self.swap:
-            first = [(i, i ^ 1) for i in range(n)]
-            second = [(i, (i + 1) % n if i % 2 else (i - 1) % n) for i in range(n)]
-            got = lax.ppermute(messages[1], self.axis, second)
-            return [lax.ppermute(messages[0], self.axis, first), got]
         up = [(i, (i + 1) % n) for i in range(n)]
         if n == 2:
             return [lax.ppermute(messages[0], self.axis, up)]
         down = [(j, i) for i, j in up]
-        return [lax.ppermute(messages[0], self.axis, up), lax.ppermute(messages[1], self.axis, down)]
+        got = lax.ppermute(messages[0], self.axis, up)
+        return [got, lax.ppermute(messages[1], self.axis, down)]
 
 
 def to_lev(message, m):
@@ -144,8 +128,8 @@
     copies[2].wait()
     both_x[0, 2] = u[:, ni - 1, :]
     both_x[1, 2] = u[:, 0, :]
-    hx.write(mx, both_x, lax.axis_index("gx") % 2 == 0)
-    hy.write(my, both_y, lax.axis_index("gy") % 2 == 0)
+    hx.write(mx, both_x)
+    hy.write(my, both_y)
     for copy in copies[3:]:
         copy.wait()
 
@@ -340,24 +324,23 @@
     depth, ni, nj = part0.shape
     last, half, per = depth - 1, depth // 2, nj // ni
     group = lax.axis_index("lev")
-    even_x, even_y = lax.axis_index("gx") % 2 == 0, lax.axis_index("gy") % 2 == 0
     if paired and first:
         condense(group, own_s, mate_s, cf)
 
-    u_lo = hx.low(rx, 2, even_x) if first else uh[0]
-    u_hi = hx.high(rx, 2, even_x) if first else uh[1]
-    u_lo = u_lo - H_STEP * (hx.down(ox, 0, even_x) - hx.low(rx, 0, even_x))
-    u_hi = u_hi - H_STEP * (hx.high(rx, 1, even_x) - hx.up(ox, 1, even_x))
-    u_first, u_last = H_STEP * hx.low(rx, 1, even_x), -H_STEP * hx.high(rx, 0, even_x)
+    u_lo = hx.low(rx, 2) if first else uh[0]
+    u_hi = hx.high(rx, 2) if first else uh[1]
+    u_lo = u_lo - H_STEP * (hx.down(ox, 0) - hx.low(rx, 0))
+    u_hi = u_hi - H_STEP * (hx.high(rx, 1) - hx.up(ox, 1))
+    u_first, u_last = H_STEP * hx.low(rx, 1), -H_STEP * hx.high(rx, 0)
     uc[0], uc[1] = u_first, u_last
-    v_lo = hy.low(ry, 2, even_y) if first else vh[0]
-    v_hi = hy.high(ry, 2, even_y) if first else vh[1]
-    v_lo = v_lo - H_STEP * (hy.down(oy, 0, even_y) - hy.low(ry, 0, even_y))
-    v_hi = v_hi - H_STEP * (hy.high(ry, 1, even_y) - hy.up(oy, 1, even_y))
+    v_lo = hy.low(ry, 2) if first else vh[0]
+    v_hi = hy.high(ry, 2) if first else vh[1]
+    v_lo = v_lo - H_STEP * (hy.down(oy, 0) - hy.low(ry, 0))
+    v_hi = v_hi - H_STEP * (hy.high(ry, 1) - hy.up(oy, 1))
     if not final:
         uh_out[0], uh_out[1] = u_lo, u_hi
         vh_out[0], vh_out[1] = v_lo, v_hi
-    v_first, v_last = H_STEP * hy.low(ry, 1, even_y), -H_STEP * hy.high(ry, 0, even_y)
+    v_first, v_last = H_STEP * hy.low(ry, 1), -H_STEP * hy.high(ry, 0)
     vc[0], vc[1] = v_first, v_last
     edges = ((0, D_STEP * u_lo), (1, D_STEP * u_first), (ni - 2, -D_STEP * u_last), (ni - 1, -D_STEP * u_hi))
     for n, (_, plane) in enumerate(edges):
@@ -532,8 +515,8 @@
         w = level(k, w)
         if (k + 1) % per == 0:
             pack_pressure(press_out, both_x, both_y, k // per)
-    hx.write(mx, both_x, lax.axis_index("gx") % 2 == 0)
-    hy.write(my, both_y, lax.axis_index("gy") % 2 == 0)
+    hx.write(mx, both_x)
+    hy.write(my, both_y)
 
 
 def body(zonal, meridional, vertical, pressure, coupling, surface, lid_flag):

time: 43.6 us -> 41.8 us (0.959)
  waiting for transfers between devices: 13.9 us -> 9.85 us
  starting transfers between devices: 20.6 us -> 22.9 us
    ppermute x6, waiting for transfers between devices: 6.96 us -> 3.04 us  [the longest x3 3.03 us: exchange(): got = lax.ppermute(messages[0], self.axis, up)]
    ppermute x6, starting transfers between devices: 9.29 us -> 11.5 us  [the longest x3 7.63 us: exchange(): return [got, lax.ppermute(messages[1], self.axis, down)]]
  transfers between devices with their start and end apart: 19 -> 19, of which waited for: 10 -> 8; matrix products, arithmetic and copies ran while one was open for 0% -> 0% of each run, Pallas kernels for 8% -> 8%
where the time goes in v2:
time: 41.8 us; the launch traced here: 41.7 us
  starting transfers between devices  22.9 us (55%)
  waiting for transfers between devices  9.85 us (24%)
  Pallas kernels  8.1 us (19%)
  between operations  0.76 us (2%)
    pallas_call x12, Pallas kernels, call(): pl.pallas_call(kernel, out_shape=[jax.ShapeDtypeStruct(s, types[n] if n <...  8.1 us
    ppermute x3, starting transfers between devices, exchange(): return [got, lax.ppermute(messages[1], self.axis, down)]  7.63 us
    ppermute x10, waiting for transfers between devices, to_lev(): return lax.ppermute(message, 'lev', [(i, i ^ m) for i in range(n)])  6.81 us
    ppermute x10, starting transfers between devices, to_lev(): return lax.ppermute(message, 'lev', [(i, i ^ m) for i in range(n)])  6.11 us
    ppermute x3, starting transfers between devices, exchange(): return [lax.ppermute(messages[0], self.axis, up)]  5.3 us
    ppermute x3, starting transfers between devices, exchange(): got = lax.ppermute(messages[0], self.axis, up)  3.89 us
    ppermute x3, waiting for transfers between devices, exchange(): got = lax.ppermute(messages[0], self.axis, up)  3.03 us
  transfers between devices with their start and end apart: 19, of which 8 were waited for; matrix products, arithmetic and copies ran while one was open for 0% of the time, Pallas kernels for 8%

profile of v2, /device:TPU:0, one launch (start us, length us, event | category | flops | bytes accessed | tf_op | source)
XLA Modules:
  0.0 41.7 jit_solution(1961874104807227098)
XLA Ops:
  0.7 1.6 %shard_map.102 = (f32[32,32,128]{2,1,0:T(8,128)S(1)}, f32[32,32,128]{2,1,0:T(8,128)S(1)}, f32[32,32,128]{2,1,0:T(8,128)S(1)}, f32[6,32,128]{2,1,0:T(8,128)S(1)},...) custom-call(f32[32,32,128]{2,1,0:T(8,128)} %refs_0_.1, f32[32,32,128]{2,1,0:T(8,128)} %refs_1_.2, f32[32,32,128]{2,1,0:T(8,128)} %refs_2_.1), custom_call_target="tpu_custom_call" | custom-call | tf_op jit(solution)/shard_map/pallas_call | solution.py:24
  2.2 3.0 %collective-permute-start = (f32[6,32,128]{2,1,0:T(8,128)S(1)}, f32[6,32,128]{2,1,0:T(8,128)S(1)}, u32[]{:S(2)}, u32[]{:S(2)}) collective-permute-start(f32[6,32,128]{2,1,0:T(8,128)S(1)} %get-tuple-element.73.refs_4_), channel_id=1, source_target_pairs={{0,16},{16,0},{1,17},{17,1},{2,18},{18,2},{3,19},{19,3},{4,20},{20... | collective-permute-start | bytes 294920 | tf_op jit(solution)/shard_map/ppermute | solution.py:74
  5.3 0.3 shard_map.104
  5.6 0.1 collective-permute-start.3
  5.6 1.6 %collective-permute-start.1 = (f32[3,8,128]{2,1,0:T(8,128)S(1)}, f32[3,8,128]{2,1,0:T(8,128)S(1)}, u32[]{:S(2)}, u32[]{:S(2)}) collective-permute-start(f32[3,8,128]{2,1,0:T(8,128)S(1)} %get-tuple-element.74.refs_5_), channel_id=1, source_target_pairs={{0,4},{4,8},{8,12},{12,0},{1,5},{5,9},{9,13},{13,1},{2,6},{6,10},{... | collective-permute-start | bytes 36872 | tf_op jit(solution)/shard_map/ppermute | solution.py:76
  7.3 2.2 %collective-permute-start.2 = (f32[3,8,128]{2,1,0:T(8,128)S(1)}, f32[3,8,128]{2,1,0:T(8,128)S(1)}, u32[]{:S(2)}, u32[]{:S(2)}) collective-permute-start(f32[3,8,128]{2,1,0:T(8,128)S(1)} %get-tuple-element.75.refs_6_), channel_id=1, source_target_pairs={{4,0},{8,4},{12,8},{0,12},{5,1},{9,5},{13,9},{1,13},{6,2},{10,6},{... | collective-permute-start | bytes 36872 | tf_op jit(solution)/shard_map/ppermute | solution.py:77
  9.5 0.6 %shard_map.103 = (f32[32,32,128]{2,1,0:T(8,128)S(1)}, f32[32,32,128]{2,1,0:T(8,128)S(1)}, f32[32,32,128]{2,1,0:T(8,128)S(1)}) custom-call(f32[32,32,128]{2,1,0:T(8,128)S(1)} %get-tuple-element.65.refs_0_, f32[32,32,128]{2,1,0:T(8,128)S(1)} %get-tuple-element.66.refs_1_, f32[32,32,128]{2,1,0:T(8,128)S(1)} %get-tuple-element.67.refs_2_), custom_call_target="tpu_custom_call" | custom-call | tf_op jit(solution)/shard_map/pallas_call | solution.py:24
  10.1 1.2 %collective-permute-done.1.refs_8_ = f32[3,8,128]{2,1,0:T(8,128)S(1)} collective-permute-done((f32[3,8,128]{2,1,0:T(8,128)S(1)}, f32[3,8,128]{2,1,0:T(8,128)S(1)}, u32[]{:S(2)}, u32[]{:S(2)}) %collective-permute-start.1) | collective-permute-done | bytes 12320 | tf_op jit(solution)/shard_map/ppermute | solution.py:76
  11.3 0.0 collective-permute-done.2.refs_9_
  11.3 0.0 collective-permute-done.3.refs_11_
  11.3 0.0 collective-permute-done.refs_7_
  11.3 0.4 %shard_map.105 = (f32[32,32,128]{2,1,0:T(8,128)S(1)}, f32[32,32,128]{2,1,0:T(8,128)S(1)}, f32[4,32,128]{2,1,0:T(8,128)S(1)}, f32[2,32,128]{2,1,0:T(8,128)S(1)}, ...) custom-call(f32[32,32,128]{2,1,0:T(8,128)S(1)} %get-tuple-element.70, ...), custom_call_target="tpu_custom_call" | custom-call | tf_op jit(solution)/shard_map/pallas_call | solution.py:24
  11.8 1.6 %collective-permute-start.5 = (f32[4,32,128]{2,1,0:T(8,128)S(1)}, f32[4,32,128]{2,1,0:T(8,128)S(1)}, u32[]{:S(2)}, u32[]{:S(2)}) collective-permute-start(f32[4,32,128]{2,1,0:T(8,128)S(1)} %get-tuple-element.82), channel_id=1, source_target_pairs={{0,2},{1,3},{2,0},{3,1},{4,6},{5,7},{6,4},{7,5},{8,10},{9,11},{10,... | collective-permute-start | bytes 196616 | tf_op jit(solution)/shard_map/ppermute | solution.py:83
  13.3 0.0 collective-permute-start.4
  13.3 0.6 %collective-permute-start.6 = (f32[2,32,128]{2,1,0:T(8,128)S(1)}, f32[2,32,128]{2,1,0:T(8,128)S(1)}, u32[]{:S(2)}, u32[]{:S(2)}) collective-permute-start(f32[2,32,128]{2,1,0:T(8,128)S(1)} %get-tuple-element.83), channel_id=1, source_target_pairs={{0,3},{1,2},{2,1},{3,0},{4,7},{5,6},{6,5},{7,4},{8,11},{9,10},{10,... | collective-permute-start | bytes 98312 | tf_op jit(solution)/shard_map/ppermute | solution.py:83
  14.0 2.7 %collective-permute-done.6.refs_7_ = f32[2,32,128]{2,1,0:T(8,128)S(1)} collective-permute-done((f32[2,32,128]{2,1,0:T(8,128)S(1)}, f32[2,32,128]{2,1,0:T(8,128)S(1)}, u32[]{:S(2)}, u32[]{:S(2)}) %collective-permute-start.6) | collective-permute-done | bytes 32800 | tf_op jit(solution)/shard_map/ppermute | solution.py:83
  16.7 0.0 collective-permute-done.4.refs_5_
  16.7 0.3 shard_map.106
  17.0 0.6 %collective-permute-start.7 = (f32[4,32,128]{2,1,0:T(8,128)S(1)}, f32[4,32,128]{2,1,0:T(8,128)S(1)}, u32[]{:S(2)}, u32[]{:S(2)}) collective-permute-start(f32[4,32,128]{2,1,0:T(8,128)S(1)} %get-tuple-element.92.refs_4_), channel_id=1, source_target_pairs={{0,16},{16,0},{1,17},{17,1},{2,18},{18,2},{3,19},{19,3},{4,20},{20... | collective-permute-start | bytes 196616 | tf_op jit(solution)/shard_map/ppermute | solution.py:74
  17.6 1.2 %collective-permute-start.8 = (f32[2,8,128]{2,1,0:T(8,128)S(1)}, f32[2,8,128]{2,1,0:T(8,128)S(1)}, u32[]{:S(2)}, u32[]{:S(2)}) collective-permute-start(f32[2,8,128]{2,1,0:T(8,128)S(1)} %get-tuple-element.93.refs_5_), channel_id=1, source_target_pairs={{0,4},{4,8},{8,12},{12,0},{1,5},{5,9},{9,13},{13,1},{2,6},{6,10},{... | collective-permute-start | bytes 24584 | tf_op jit(solution)/shard_map/ppermute | solution.py:76
  18.9 2.6 %collective-permute-start.9 = (f32[2,8,128]{2,1,0:T(8,128)S(1)}, f32[2,8,128]{2,1,0:T(8,128)S(1)}, u32[]{:S(2)}, u32[]{:S(2)}) collective-permute-start(f32[2,8,128]{2,1,0:T(8,128)S(1)} %get-tuple-element.94.refs_6_), channel_id=1, source_target_pairs={{4,0},{8,4},{12,8},{0,12},{5,1},{9,5},{13,9},{1,13},{6,2},{10,6},{... | collective-permute-start | bytes 24584 | tf_op jit(solution)/shard_map/ppermute | solution.py:77
  21.5 0.7 %shard_map.107 = (f32[32,32,128]{2,1,0:T(8,128)S(1)}, f32[32,32,128]{2,1,0:T(8,128)S(1)}, f32[32,32,128]{2,1,0:T(8,128)S(1)}) custom-call(f32[32,32,128]{2,1,0:T(8,128)S(1)} %get-tuple-element.68.refs_0_, f32[32,32,128]{2,1,0:T(8,128)S(1)} %get-tuple-element.69.refs_1_, f32[32,32,128]{2,1,0:T(8,128)S(1)} %get-tuple-element.85.refs_2_, ...), custom_call_target="tpu_custom_call" | custom-call | tf_op jit(solution)/shard_map/pallas_call | solution.py:24
  22.2 0.9 %collective-permute-done.8.refs_8_ = f32[2,8,128]{2,1,0:T(8,128)S(1)} collective-permute-done((f32[2,8,128]{2,1,0:T(8,128)S(1)}, f32[2,8,128]{2,1,0:T(8,128)S(1)}, u32[]{:S(2)}, u32[]{:S(2)}) %collective-permute-start.8) | collective-permute-done | bytes 8224 | tf_op jit(solution)/shard_map/ppermute | solution.py:76
  23.1 0.0 collective-permute-done.9.refs_9_
  23.1 0.4 %shard_map.108 = (f32[32,32,128]{2,1,0:T(8,128)S(1)}, f32[32,32,128]{2,1,0:T(8,128)S(1)}, f32[4,32,128]{2,1,0:T(8,128)S(1)}, f32[2,32,128]{2,1,0:T(8,128)S(1)}, ...) custom-call(f32[32,32,128]{2,1,0:T(8,128)S(1)} %get-tuple-element.90, ...), custom_call_target="tpu_custom_call" | custom-call | tf_op jit(solution)/shard_map/pallas_call | solution.py:24
  23.5 0.1 collective-permute-start.10
  23.6 1.2 %collective-permute-start.11 = (f32[2,32,128]{2,1,0:T(8,128)S(1)}, f32[2,32,128]{2,1,0:T(8,128)S(1)}, u32[]{:S(2)}, u32[]{:S(2)}) collective-permute-start(f32[2,32,128]{2,1,0:T(8,128)S(1)} %get-tuple-element.101), channel_id=1, source_target_pairs={{0,2},{1,3},{2,0},{3,1},{4,6},{5,7},{6,4},{7,5},{8,10},{9,11},{10,... | collective-permute-start | bytes 98312 | tf_op jit(solution)/shard_map/ppermute | solution.py:83
  24.8 0.7 %collective-permute-start.12 = (f32[2,32,128]{2,1,0:T(8,128)S(1)}, f32[2,32,128]{2,1,0:T(8,128)S(1)}, u32[]{:S(2)}, u32[]{:S(2)}) collective-permute-start(f32[2,32,128]{2,1,0:T(8,128)S(1)} %get-tuple-element.102), channel_id=1, source_target_pairs={{0,3},{1,2},{2,1},{3,0},{4,7},{5,6},{6,5},{7,4},{8,11},{9,10},{10,... | collective-permute-start | bytes 98312 | tf_op jit(solution)/shard_map/ppermute | solution.py:83
  25.5 2.1 %collective-permute-done.11.refs_6_ = f32[2,32,128]{2,1,0:T(8,128)S(1)} collective-permute-done((f32[2,32,128]{2,1,0:T(8,128)S(1)}, f32[2,32,128]{2,1,0:T(8,128)S(1)}, u32[]{:S(2)}, u32[]{:S(2)}) %collective-permute-start.11) | collective-permute-done | bytes 32800 | tf_op jit(solution)/shard_map/ppermute | solution.py:83
  27.6 0.5 %collective-permute-done.12.refs_7_ = f32[2,32,128]{2,1,0:T(8,128)S(1)} collective-permute-done((f32[2,32,128]{2,1,0:T(8,128)S(1)}, f32[2,32,128]{2,1,0:T(8,128)S(1)}, u32[]{:S(2)}, u32[]{:S(2)}) %collective-permute-start.12) | collective-permute-done | bytes 32800 | tf_op jit(solution)/shard_map/ppermute | solution.py:83
  28.1 0.0 collective-permute-done.10.refs_5_
  28.1 0.3 shard_map.109
  28.5 1.7 %collective-permute-start.13 = (f32[4,32,128]{2,1,0:T(8,128)S(1)}, f32[4,32,128]{2,1,0:T(8,128)S(1)}, u32[]{:S(2)}, u32[]{:S(2)}) collective-permute-start(f32[4,32,128]{2,1,0:T(8,128)S(1)} %get-tuple-element.110.refs_4_), channel_id=1, source_target_pairs={{0,16},{16,0},{1,17},{17,1},{2,18},{18,2},{3,19},{19,3},{4,20},{20... | collective-permute-start | bytes 196616 | tf_op jit(solution)/shard_map/ppermute | solution.py:74
  30.1 1.0 %collective-permute-start.14 = (f32[2,8,128]{2,1,0:T(8,128)S(1)}, f32[2,8,128]{2,1,0:T(8,128)S(1)}, u32[]{:S(2)}, u32[]{:S(2)}) collective-permute-start(f32[2,8,128]{2,1,0:T(8,128)S(1)} %get-tuple-element.111.refs_5_), channel_id=1, source_target_pairs={{0,4},{4,8},{8,12},{12,0},{1,5},{5,9},{9,13},{13,1},{2,6},{6,10},{... | collective-permute-start | bytes 24584 | tf_op jit(solution)/shard_map/ppermute | solution.py:76
  31.1 2.8 %collective-permute-start.15 = (f32[2,8,128]{2,1,0:T(8,128)S(1)}, f32[2,8,128]{2,1,0:T(8,128)S(1)}, u32[]{:S(2)}, u32[]{:S(2)}) collective-permute-start(f32[2,8,128]{2,1,0:T(8,128)S(1)} %get-tuple-element.112.refs_6_), channel_id=1, source_target_pairs={{4,0},{8,4},{12,8},{0,12},{5,1},{9,5},{13,9},{1,13},{6,2},{10,6},{... | collective-permute-start | bytes 24584 | tf_op jit(solution)/shard_map/ppermute | solution.py:77
  34.0 0.7 %shard_map.110 = (f32[32,32,128]{2,1,0:T(8,128)S(1)}, f32[32,32,128]{2,1,0:T(8,128)S(1)}, f32[32,32,128]{2,1,0:T(8,128)S(1)}) custom-call(f32[32,32,128]{2,1,0:T(8,128)S(1)} %get-tuple-element.88.refs_0_, f32[32,32,128]{2,1,0:T(8,128)S(1)} %get-tuple-element.89.refs_1_, f32[32,32,128]{2,1,0:T(8,128)S(1)} %get-tuple-element.103.refs_2_, ...), custom_call_target="tpu_custom_call" | custom-call | tf_op jit(solution)/shard_map/pallas_call | solution.py:24
  34.6 0.9 %collective-permute-done.14.refs_8_ = f32[2,8,128]{2,1,0:T(8,128)S(1)} collective-permute-done((f32[2,8,128]{2,1,0:T(8,128)S(1)}, f32[2,8,128]{2,1,0:T(8,128)S(1)}, u32[]{:S(2)}, u32[]{:S(2)}) %collective-permute-start.14) | collective-permute-done | bytes 8224 | tf_op jit(solution)/shard_map/ppermute | solution.py:76
  35.6 0.0 collective-permute-done.15.refs_9_
  35.6 0.0 collective-permute-done.13.refs_7_
  35.6 0.4 %shard_map.111 = (f32[32,32,128]{2,1,0:T(8,128)S(1)}, f32[32,32,128]{2,1,0:T(8,128)S(1)}, f32[4,32,128]{2,1,0:T(8,128)S(1)}, f32[2,32,128]{2,1,0:T(8,128)S(1)}, ...) custom-call(f32[32,32,128]{2,1,0:T(8,128)S(1)} %get-tuple-element.108.refs_0_, ...), custom_call_target="tpu_custom_call" | custom-call | tf_op jit(solution)/shard_map/pallas_call | solution.py:24
  36.0 0.1 collective-permute-start.16
  36.1 1.1 %collective-permute-start.17 = (f32[2,32,128]{2,1,0:T(8,128)S(1)}, f32[2,32,128]{2,1,0:T(8,128)S(1)}, u32[]{:S(2)}, u32[]{:S(2)}) collective-permute-start(f32[2,32,128]{2,1,0:T(8,128)S(1)} %get-tuple-element.122), channel_id=1, source_target_pairs={{0,2},{1,3},{2,0},{3,1},{4,6},{5,7},{6,4},{7,5},{8,10},{9,11},{10,... | collective-permute-start | bytes 98312 | tf_op jit(solution)/shard_map/ppermute | solution.py:83
  37.2 0.8 %collective-permute-start.18 = (f32[2,32,128]{2,1,0:T(8,128)S(1)}, f32[2,32,128]{2,1,0:T(8,128)S(1)}, u32[]{:S(2)}, u32[]{:S(2)}) collective-permute-start(f32[2,32,128]{2,1,0:T(8,128)S(1)} %get-tuple-element.123), channel_id=1, source_target_pairs={{0,3},{1,2},{2,1},{3,0},{4,7},{5,6},{6,5},{7,4},{8,11},{9,10},{10,... | collective-permute-start | bytes 98312 | tf_op jit(solution)/shard_map/ppermute | solution.py:83
  37.9 1.2 %shard_map.112 = (f32[32,32,128]{2,1,0:T(8,128)}, f32[32,32,128]{2,1,0:T(8,128)}) custom-call(f32[32,32,128]{2,1,0:T(8,128)S(1)} %get-tuple-element.106.zonal, f32[32,32,128]{2,1,0:T(8,128)S(1)} %get-tuple-element.107.merid, f32[2,32,128]{2,1,0:T(8,128)S(1)} %get-tuple-element.115.uc, f32[2,8,128]{2,1,0:T(8,128)S(1)} %get-tuple-element.116.vc), custom_call_target="tpu_custom_call" | custom-call | tf_op jit(solution)/shard_map/pallas_call | solution.py:24
  39.1 0.9 %collective-permute-done.17.refs_6_ = f32[2,32,128]{2,1,0:T(8,128)S(1)} collective-permute-done((f32[2,32,128]{2,1,0:T(8,128)S(1)}, f32[2,32,128]{2,1,0:T(8,128)S(1)}, u32[]{:S(2)}, u32[]{:S(2)}) %collective-permute-start.17) | collective-permute-done | bytes 32800 | tf_op jit(solution)/shard_map/ppermute | solution.py:83
  40.1 0.5 %collective-permute-done.18.refs_7_ = f32[2,32,128]{2,1,0:T(8,128)S(1)} collective-permute-done((f32[2,32,128]{2,1,0:T(8,128)S(1)}, f32[2,32,128]{2,1,0:T(8,128)S(1)}, u32[]{:S(2)}, u32[]{:S(2)}) %collective-permute-start.18) | collective-permute-done | bytes 32800 | tf_op jit(solution)/shard_map/ppermute | solution.py:83
  40.6 0.0 collective-permute-done.16.refs_5_
  40.6 1.1 %shard_map.113 = (f32[32,32,128]{2,1,0:T(8,128)}, f32[32,32,128]{2,1,0:T(8,128)}) custom-call(f32[32,32,128]{2,1,0:T(8,128)S(1)} %get-tuple-element.119.refs_0_, f32[32,32,128]{2,1,0:T(8,128)S(1)} %get-tuple-element.120.refs_1_, f32[32,32,128]{2,1,0:T(8,128)S(1)} %get-tuple-element.79.refs_2_, f32[32,32,128]{2,1,0:T(8,128)S(1)} %get-tuple-element.80.refs_3_, ...), custom_call_target="tpu_custom_call" | custom-call | tf_op jit(solution)/shard_map/pallas_call | solution.py:24
  (10 shorter events, 0.0 us)
Async XLA Ops:
  0.6 4.6 %copy-start.3 = (s32[32,128]{1,0:T(8,128)S(1)}, s32[32,128]{1,0:T(8,128)}, u32[]{:S(2)}) copy-start(s32[32,128]{1,0:T(8,128)} %lid.1) | copy-start | bytes 49156
  0.6 4.6 %copy-start.2 = (s32[32,128]{1,0:T(8,128)S(1)}, s32[32,128]{1,0:T(8,128)}, u32[]{:S(2)}) copy-start(s32[32,128]{1,0:T(8,128)} %surface.1) | copy-start | bytes 49156
  0.7 4.6 %copy-start.1 = (f32[32,32,128]{2,1,0:T(8,128)S(1)}, f32[32,32,128]{2,1,0:T(8,128)}, u32[]{:S(2)}) copy-start(f32[32,32,128]{2,1,0:T(8,128)} %c.1) | copy-start | bytes 1572868
  2.2 9.1 %collective-permute-start = (f32[6,32,128]{2,1,0:T(8,128)S(1)}, f32[6,32,128]{2,1,0:T(8,128)S(1)}, u32[]{:S(2)}, u32[]{:S(2)}) collective-permute-start(f32[6,32,128]{2,1,0:T(8,128)S(1)} %get-tuple-element.73.refs_4_), channel_id=1, source_target_pairs={{0,16},{16,0},{1,17},{17,1},{2,18},{18,2},{3,19},{19,3},{4,20},{20... | collective-permute-start | bytes 294920 | tf_op jit(solution)/shard_map/ppermute | solution.py:74
  5.6 5.7 %collective-permute-start.3 = (f32[4,32,128]{2,1,0:T(8,128)S(1)}, f32[4,32,128]{2,1,0:T(8,128)S(1)}, u32[]{:S(2)}, u32[]{:S(2)}) collective-permute-start(f32[4,32,128]{2,1,0:T(8,128)S(1)} %get-tuple-element.76.refs_10_), channel_id=1, source_target_pairs={{0,1},{1,0},{2,3},{3,2},{4,5},{5,4},{6,7},{7,6},{8,9},{9,8},{10,11... | collective-permute-start | bytes 196616 | tf_op jit(solution)/shard_map/ppermute | solution.py:83
  5.6 5.6 %collective-permute-start.1 = (f32[3,8,128]{2,1,0:T(8,128)S(1)}, f32[3,8,128]{2,1,0:T(8,128)S(1)}, u32[]{:S(2)}, u32[]{:S(2)}) collective-permute-start(f32[3,8,128]{2,1,0:T(8,128)S(1)} %get-tuple-element.74.refs_5_), channel_id=1, source_target_pairs={{0,4},{4,8},{8,12},{12,0},{1,5},{5,9},{9,13},{13,1},{2,6},{6,10},{... | collective-permute-start | bytes 36872 | tf_op jit(solution)/shard_map/ppermute | solution.py:76
  7.3 4.0 %collective-permute-start.2 = (f32[3,8,128]{2,1,0:T(8,128)S(1)}, f32[3,8,128]{2,1,0:T(8,128)S(1)}, u32[]{:S(2)}, u32[]{:S(2)}) collective-permute-start(f32[3,8,128]{2,1,0:T(8,128)S(1)} %get-tuple-element.75.refs_6_), channel_id=1, source_target_pairs={{4,0},{8,4},{12,8},{0,12},{5,1},{9,5},{13,9},{1,13},{6,2},{10,6},{... | collective-permute-start | bytes 36872 | tf_op jit(solution)/shard_map/ppermute | solution.py:77
  9.5 1.8 %copy-start = (f32[32,32,128]{2,1,0:T(8,128)S(1)}, f32[32,32,128]{2,1,0:T(8,128)}, u32[]{:S(2)}) copy-start(f32[32,32,128]{2,1,0:T(8,128)} %refs_1_.3) | copy-start | bytes 1572868
  11.8 4.9 %collective-permute-start.5 = (f32[4,32,128]{2,1,0:T(8,128)S(1)}, f32[4,32,128]{2,1,0:T(8,128)S(1)}, u32[]{:S(2)}, u32[]{:S(2)}) collective-permute-start(f32[4,32,128]{2,1,0:T(8,128)S(1)} %get-tuple-element.82), channel_id=1, source_target_pairs={{0,2},{1,3},{2,0},{3,1},{4,6},{5,7},{6,4},{7,5},{8,10},{9,11},{10,... | collective-permute-start | bytes 196616 | tf_op jit(solution)/shard_map/ppermute | solution.py:83
  13.3 3.3 %collective-permute-start.4 = (f32[4,32,128]{2,1,0:T(8,128)S(1)}, f32[4,32,128]{2,1,0:T(8,128)S(1)}, u32[]{:S(2)}, u32[]{:S(2)}) collective-permute-start(f32[4,32,128]{2,1,0:T(8,128)S(1)} %get-tuple-element.81.refs_4_), channel_id=1, source_target_pairs={{0,1},{1,0},{2,3},{3,2},{4,5},{5,4},{6,7},{7,6},{8,9},{9,8},{10,11... | collective-permute-start | bytes 196616 | tf_op jit(solution)/shard_map/ppermute | solution.py:83
  13.3 3.3 %collective-permute-start.6 = (f32[2,32,128]{2,1,0:T(8,128)S(1)}, f32[2,32,128]{2,1,0:T(8,128)S(1)}, u32[]{:S(2)}, u32[]{:S(2)}) collective-permute-start(f32[2,32,128]{2,1,0:T(8,128)S(1)} %get-tuple-element.83), channel_id=1, source_target_pairs={{0,3},{1,2},{2,1},{3,0},{4,7},{5,6},{6,5},{7,4},{8,11},{9,10},{10,... | collective-permute-start | bytes 98312 | tf_op jit(solution)/shard_map/ppermute | solution.py:83
  17.0 6.1 %collective-permute-start.7 = (f32[4,32,128]{2,1,0:T(8,128)S(1)}, f32[4,32,128]{2,1,0:T(8,128)S(1)}, u32[]{:S(2)}, u32[]{:S(2)}) collective-permute-start(f32[4,32,128]{2,1,0:T(8,128)S(1)} %get-tuple-element.92.refs_4_), channel_id=1, source_target_pairs={{0,16},{16,0},{1,17},{17,1},{2,18},{18,2},{3,19},{19,3},{4,20},{20... | collective-permute-start | bytes 196616 | tf_op jit(solution)/shard_map/ppermute | solution.py:74
  17.6 5.4 %collective-permute-start.8 = (f32[2,8,128]{2,1,0:T(8,128)S(1)}, f32[2,8,128]{2,1,0:T(8,128)S(1)}, u32[]{:S(2)}, u32[]{:S(2)}) collective-permute-start(f32[2,8,128]{2,1,0:T(8,128)S(1)} %get-tuple-element.93.refs_5_), channel_id=1, source_target_pairs={{0,4},{4,8},{8,12},{12,0},{1,5},{5,9},{9,13},{13,1},{2,6},{6,10},{... | collective-permute-start | bytes 24584 | tf_op jit(solution)/shard_map/ppermute | solution.py:76
  18.9 4.2 %collective-permute-start.9 = (f32[2,8,128]{2,1,0:T(8,128)S(1)}, f32[2,8,128]{2,1,0:T(8,128)S(1)}, u32[]{:S(2)}, u32[]{:S(2)}) collective-permute-start(f32[2,8,128]{2,1,0:T(8,128)S(1)} %get-tuple-element.94.refs_6_), channel_id=1, source_target_pairs={{4,0},{8,4},{12,8},{0,12},{5,1},{9,5},{13,9},{1,13},{6,2},{10,6},{... | collective-permute-start | bytes 24584 | tf_op jit(solution)/shard_map/ppermute | solution.py:77
  23.5 4.6 %collective-permute-start.10 = (f32[4,32,128]{2,1,0:T(8,128)S(1)}, f32[4,32,128]{2,1,0:T(8,128)S(1)}, u32[]{:S(2)}, u32[]{:S(2)}) collective-permute-start(f32[4,32,128]{2,1,0:T(8,128)S(1)} %get-tuple-element.100.refs_4_), channel_id=1, source_target_pairs={{0,1},{1,0},{2,3},{3,2},{4,5},{5,4},{6,7},{7,6},{8,9},{9,8},{10,11... | collective-permute-start | bytes 196616 | tf_op jit(solution)/shard_map/ppermute | solution.py:83
  23.6 4.0 %collective-permute-start.11 = (f32[2,32,128]{2,1,0:T(8,128)S(1)}, f32[2,32,128]{2,1,0:T(8,128)S(1)}, u32[]{:S(2)}, u32[]{:S(2)}) collective-permute-start(f32[2,32,128]{2,1,0:T(8,128)S(1)} %get-tuple-element.101), channel_id=1, source_target_pairs={{0,2},{1,3},{2,0},{3,1},{4,6},{5,7},{6,4},{7,5},{8,10},{9,11},{10,... | collective-permute-start | bytes 98312 | tf_op jit(solution)/shard_map/ppermute | solution.py:83
  24.8 3.4 %collective-permute-start.12 = (f32[2,32,128]{2,1,0:T(8,128)S(1)}, f32[2,32,128]{2,1,0:T(8,128)S(1)}, u32[]{:S(2)}, u32[]{:S(2)}) collective-permute-start(f32[2,32,128]{2,1,0:T(8,128)S(1)} %get-tuple-element.102), channel_id=1, source_target_pairs={{0,3},{1,2},{2,1},{3,0},{4,7},{5,6},{6,5},{7,4},{8,11},{9,10},{10,... | collective-permute-start | bytes 98312 | tf_op jit(solution)/shard_map/ppermute | solution.py:83
  28.5 7.1 %collective-permute-start.13 = (f32[4,32,128]{2,1,0:T(8,128)S(1)}, f32[4,32,128]{2,1,0:T(8,128)S(1)}, u32[]{:S(2)}, u32[]{:S(2)}) collective-permute-start(f32[4,32,128]{2,1,0:T(8,128)S(1)} %get-tuple-element.110.refs_4_), channel_id=1, source_target_pairs={{0,16},{16,0},{1,17},{17,1},{2,18},{18,2},{3,19},{19,3},{4,20},{20... | collective-permute-start | bytes 196616 | tf_op jit(solution)/shard_map/ppermute | solution.py:74
  30.1 5.4 %collective-permute-start.14 = (f32[2,8,128]{2,1,0:T(8,128)S(1)}, f32[2,8,128]{2,1,0:T(8,128)S(1)}, u32[]{:S(2)}, u32[]{:S(2)}) collective-permute-start(f32[2,8,128]{2,1,0:T(8,128)S(1)} %get-tuple-element.111.refs_5_), channel_id=1, source_target_pairs={{0,4},{4,8},{8,12},{12,0},{1,5},{5,9},{9,13},{13,1},{2,6},{6,10},{... | collective-permute-start | bytes 24584 | tf_op jit(solution)/shard_map/ppermute | solution.py:76
  31.1 4.4 %collective-permute-start.15 = (f32[2,8,128]{2,1,0:T(8,128)S(1)}, f32[2,8,128]{2,1,0:T(8,128)S(1)}, u32[]{:S(2)}, u32[]{:S(2)}) collective-permute-start(f32[2,8,128]{2,1,0:T(8,128)S(1)} %get-tuple-element.112.refs_6_), channel_id=1, source_target_pairs={{4,0},{8,4},{12,8},{0,12},{5,1},{9,5},{13,9},{1,13},{6,2},{10,6},{... | collective-permute-start | bytes 24584 | tf_op jit(solution)/shard_map/ppermute | solution.py:77
  36.0 4.5 %collective-permute-start.16 = (f32[4,32,128]{2,1,0:T(8,128)S(1)}, f32[4,32,128]{2,1,0:T(8,128)S(1)}, u32[]{:S(2)}, u32[]{:S(2)}) collective-permute-start(f32[4,32,128]{2,1,0:T(8,128)S(1)} %get-tuple-element.121.refs_4_), channel_id=1, source_target_pairs={{0,1},{1,0},{2,3},{3,2},{4,5},{5,4},{6,7},{7,6},{8,9},{9,8},{10,11... | collective-permute-start | bytes 196616 | tf_op jit(solution)/shard_map/ppermute | solution.py:83
  36.1 4.0 %collective-permute-start.17 = (f32[2,32,128]{2,1,0:T(8,128)S(1)}, f32[2,32,128]{2,1,0:T(8,128)S(1)}, u32[]{:S(2)}, u32[]{:S(2)}) collective-permute-start(f32[2,32,128]{2,1,0:T(8,128)S(1)} %get-tuple-element.122), channel_id=1, source_target_pairs={{0,2},{1,3},{2,0},{3,1},{4,6},{5,7},{6,4},{7,5},{8,10},{9,11},{10,... | collective-permute-start | bytes 98312 | tf_op jit(solution)/shard_map/ppermute | solution.py:83
  37.2 3.4 %collective-permute-start.18 = (f32[2,32,128]{2,1,0:T(8,128)S(1)}, f32[2,32,128]{2,1,0:T(8,128)S(1)}, u32[]{:S(2)}, u32[]{:S(2)}) collective-permute-start(f32[2,32,128]{2,1,0:T(8,128)S(1)} %get-tuple-element.123), channel_id=1, source_target_pairs={{0,3},{1,2},{2,1},{3,0},{4,7},{5,6},{6,5},{7,4},{8,11},{9,10},{10,... | collective-permute-start | bytes 98312 | tf_op jit(solution)/shard_map/ppermute | solution.py:83
